TPU v7x, 256 devices: a whole 4x4x8 slice. The times are simulated.
256 devices in a mesh: seq: 64 (over y, z, core), head: 4 (over x).
Axes of the slice: x: 4, y: 4, z: 8, core: 2. Of those that a mesh axis runs over, the one named last changes fastest.
Arguments:
- query_rows: bfloat16 [8192, 2048], P('seq', 'head'), may hold values from -6 to 6
- key_rows: bfloat16 [8192, 2048], P('seq', 'head'), may hold values from -0.52734375 to 0.52734375
- value_rows: bfloat16 [8192, 2048], P('seq', 'head'), may hold values from -6 to 6
- ridge_reg: float32 [16], P('head'), may hold values from 0.5 to 4
- out_weight: bfloat16 [2048, 2048], P('head'), may hold values from -0.125 to 0.125
- out_grad: bfloat16 [8192, 2048], P('seq', 'head'), may hold values from -8 to 8
- doc_ids: int32 [8192], P('seq'), may hold values from 0 to 7, never falling along the last dimension, each value on 1 to 4096 neighbouring positions
Outputs:
- layer_out: bfloat16 [8192, 2048], P('seq', 'head')
- grad_queries: bfloat16 [8192, 2048], P('seq', 'head')
- grad_keys: bfloat16 [8192, 2048], P('seq', 'head')
- grad_values: bfloat16 [8192, 2048], P('seq', 'head')
- grad_weight: float32 [2048, 2048], P('seq', 'head')
Inputs may be any that keep to these rules, and one draw needn't show every extreme that they name: `doc_ids`: document numbers never fall along the tokens; every number occurs, each document has 1 to 4096 tokens and one has exactly 4096.
All inputs are finite; a program needn't handle non-finite values.
Results may differ from a plain program's by a relative error of at most 0.018.
Values may be sent and summed in bfloat16 or wider, within the bound.
A program may use at most 128 MiB of HBM per device.

v0:
```python
import jax
import jax.numpy as jnp
from jax import lax
from jax.sharding import PartitionSpec as P

CG_STEPS = 4


epsilon = 1e-06


def prefix(value, axis, combine, identity, reverse):
    devices, place = (lax.axis_size(axis), lax.axis_index(axis))
    everything = jax.tree.map(
        lambda part, kind: lax.all_gather(part.astype(kind), axis),
        value,
        jax.tree.map(lambda a: jnp.bfloat16 if a.dtype == jnp.float32 else a.dtype, value),
    )
    start = jax.tree.map(
        lambda part, zero: jnp.broadcast_to(jnp.asarray(zero, part.dtype), part.shape),
        value,
        identity,
    )

    def step(k, before):
        at = devices - 1 - k if reverse else k
        reached = at > place if reverse else at < place
        new = combine(
            before, jax.tree.map(lambda part, own: part[at].astype(own.dtype), everything, value)
        )
        return jax.tree.map(lambda a, b: jnp.where(reached, a, b), new, before)

    return lax.fori_loop(0, devices, step, start)


def matmul_high(left_side, right_side):
    return jnp.dot(
        left_side, right_side, precision=lax.Precision.HIGHEST, preferred_element_type=jnp.float32
    )


def causal_mask(labels):
    length = labels.shape[0]
    row_idx = lax.broadcasted_iota(jnp.int32, (length, length), 0)
    col_idx = lax.broadcasted_iota(jnp.int32, (length, length), 1)
    return ((labels[:, None] == labels[None, :]) & (col_idx <= row_idx)).astype(jnp.float32)


def conj_solve(target, key_rows, same_doc, carried, gram_in, ridge_reg):
    solution = jnp.zeros_like(target)
    residual = target
    direction = target
    res_sq = jnp.sum(residual * residual, axis=1, keepdims=True)
    for number in range(CG_STEPS):
        scores = matmul_high(direction, key_rows.T) * same_doc
        applied = (
            carried[:, None] * matmul_high(direction, gram_in)
            + matmul_high(scores, key_rows)
            + ridge_reg * direction
        )
        step_size = res_sq / (jnp.sum(direction * applied, axis=1, keepdims=True) + epsilon)
        solution = solution + step_size * direction
        residual = residual - step_size * applied
        new_sq = jnp.sum(residual * residual, axis=1, keepdims=True)
        direction = residual + new_sq / (res_sq + epsilon) * direction
        res_sq = new_sq
    return solution


def head_forward(query_rows, key_rows, value_rows, same_doc, carried, gram_in, value_in, ridge_reg):
    solution = conj_solve(query_rows, key_rows, same_doc, carried, gram_in, ridge_reg)
    score_one = matmul_high(solution, key_rows.T) * same_doc
    output = carried[:, None] * matmul_high(solution, value_in.T) + matmul_high(
        score_one, value_rows
    )
    return (solution, output)


def head_dual(
    key_rows,
    value_rows,
    same_doc,
    carried,
    head_rows,
    gram_in,
    value_in,
    ridge_reg,
    solution,
    out_cot,
):
    score_two = matmul_high(out_cot, value_rows.T) * same_doc
    target = carried[:, None] * matmul_high(out_cot, value_in) + matmul_high(score_two, key_rows)
    dual_sol = conj_solve(target, key_rows, same_doc, carried, gram_in, ridge_reg)
    state_part = matmul_high(out_cot.T, head_rows[:, None] * solution)
    cross_sum = matmul_high(dual_sol.T, head_rows[:, None] * solution)
    return (dual_sol, state_part, cross_sum + cross_sum.T, score_two)


def head_grads(
    key_rows,
    value_rows,
    same_doc,
    later_rows,
    solution,
    out_cot,
    dual_sol,
    score_two,
    grad_state,
    gram_grad,
):
    score_one = matmul_high(solution, key_rows.T) * same_doc
    score_three = matmul_high(dual_sol, key_rows.T) * same_doc
    grad_v = later_rows[:, None] * matmul_high(key_rows, grad_state.T) + matmul_high(
        score_one.T, out_cot
    )
    grad_k = later_rows[:, None] * (
        matmul_high(value_rows, grad_state) - matmul_high(key_rows, gram_grad)
    )
    grad_k = (
        grad_k
        + matmul_high(score_two.T, solution)
        - matmul_high(score_one.T, dual_sol)
        - matmul_high(score_three.T, solution)
    )
    return (grad_k, grad_v)


def link_states(earlier, later):
    broken_a, label_a, gram_a, value_a = earlier
    broken_b, label_b, gram_b, value_b = later
    same_label = (label_a == label_b) | (label_a == 0) | (label_b == 0)
    broken = jnp.maximum(jnp.maximum(broken_a, broken_b), 1 - same_label.astype(jnp.int32))
    joined = (broken_b == 0) & same_label
    gram_sum = jnp.where(joined, gram_a + gram_b, gram_b)
    value_sum = jnp.where(joined, value_a + value_b, value_b)
    doc_label = jnp.where(label_b == 0, label_a, label_b)
    return (broken, doc_label, gram_sum, value_sum)


def blank_like(element):
    return tuple((jnp.zeros_like(member) for member in element))


def to_heads(array, heads_here):
    return array.astype(jnp.float32).reshape(array.shape[0], heads_here, -1).transpose(1, 0, 2)


def from_heads(array):
    return array.transpose(1, 0, 2).reshape(array.shape[1], -1)


def per_device(query_rows, key_rows, value_rows, ridge_reg, out_weight, out_grad, doc_ids):
    heads_here = ridge_reg.shape[0]
    query_h = to_heads(query_rows, heads_here)
    key_h = to_heads(key_rows, heads_here)
    value_h = to_heads(value_rows, heads_here)
    same_doc = causal_mask(doc_ids)
    broken_here = (doc_ids[0] != doc_ids[-1]).astype(jnp.int32)
    tail_rows = (doc_ids == doc_ids[-1]).astype(jnp.float32)[None, :, None]
    gram_tail = jnp.einsum(
        "hpk,hpl->hkl",
        key_h * tail_rows,
        key_h,
        precision=lax.Precision.HIGHEST,
        preferred_element_type=jnp.float32,
    )
    value_tail = jnp.einsum(
        "hpv,hpk->hvk",
        value_h * tail_rows,
        key_h,
        precision=lax.Precision.HIGHEST,
        preferred_element_type=jnp.float32,
    )
    element = (broken_here, doc_ids[-1] + 1, gram_tail, value_tail)
    incoming = prefix(element, "seq", link_states, blank_like(element), False)
    label_in = incoming[1] - 1
    gram_in = incoming[2]
    value_in = incoming[3]
    carried = (doc_ids == label_in).astype(jnp.float32)
    solution, output = jax.vmap(head_forward, in_axes=(0, 0, 0, None, None, 0, 0, 0))(
        query_h, key_h, value_h, same_doc, carried, gram_in, value_in, ridge_reg
    )
    mixed = from_heads(output).astype(jnp.bfloat16)
    partial_out = jnp.dot(mixed, out_weight, preferred_element_type=jnp.float32)
    layer_out = lax.psum_scatter(
        partial_out.astype(jnp.bfloat16), "head", scatter_dimension=1, tiled=True
    )
    cot_full = lax.all_gather(out_grad, "head", axis=1, tiled=True)
    out_cot = to_heads(
        jnp.dot(cot_full, out_weight.T, preferred_element_type=jnp.float32), heads_here
    )
    grad_weight = lax.psum_scatter(
        lax.dot_general(
            cot_full, mixed, (((0,), (0,)), ((), ())), preferred_element_type=jnp.float32
        ),
        "seq",
        scatter_dimension=0,
        tiled=True,
    )
    head_rows = (doc_ids == doc_ids[0]).astype(jnp.float32)
    dual_sol, state_part, gram_part, score_two = jax.vmap(
        head_dual, in_axes=(0, 0, None, None, None, 0, 0, 0, 0, 0)
    )(key_h, value_h, same_doc, carried, head_rows, gram_in, value_in, ridge_reg, solution, out_cot)
    back_element = (broken_here, doc_ids[0] + 1, state_part, gram_part)
    from_later = prefix(back_element, "seq", link_states, blank_like(back_element), True)
    later_rows = (doc_ids == from_later[1] - 1).astype(jnp.float32)
    grad_k, grad_v = jax.vmap(head_grads, in_axes=(0, 0, None, None, 0, 0, 0, 0, 0, 0))(
        key_h,
        value_h,
        same_doc,
        later_rows,
        solution,
        out_cot,
        dual_sol,
        score_two,
        from_later[2],
        from_later[3],
    )
    grad_queries = from_heads(dual_sol).astype(jnp.bfloat16)
    grad_keys = from_heads(grad_k).astype(jnp.bfloat16)
    grad_values = from_heads(grad_v).astype(jnp.bfloat16)
    return (layer_out, grad_queries, grad_keys, grad_values, grad_weight)


def solution(mesh):
    in_specs = (
        P("seq", "head"),
        P("seq", "head"),
        P("seq", "head"),
        P("head"),
        P("head", None),
        P("seq", "head"),
        P("seq"),
    )
    out_specs = (
        P("seq", "head"),
        P("seq", "head"),
        P("seq", "head"),
        P("seq", "head"),
        P("seq", "head"),
    )
    return jax.shard_map(
        per_device, mesh=mesh, in_specs=in_specs, out_specs=out_specs, check_vma=False
    )
```

profile of v0, /device:TPU:1, one launch (start us, length us, event | category | flops | bytes accessed | tf_op | source)
XLA Modules:
  0.0 1026.7 jit_solution(9537086225200754150)
XLA Ops:
  7.2 1.4 fusion.87
  10.9 1.8 convolution_convert_fusion.2
  13.9 1.8 convolution_convert_fusion.3
  22.8 21.9 %all-reduce.3 = (s32[64]{0:T(128)S(1)}, s32[64]{0:T(128)S(1)}, s32[64]{0:T(128)}) all-reduce(s32[64]{0:T(128)S(1)} %dynamic-update-slice, s32[64]{0:T(128)S(1)} %dynamic-update-slice.1, s32[64]{0:T(128)S(1)} %dynamic-update-slice.2), channel_id=1, replica_groups=mesh['seq'=64,'head'=4] {'seq'}, use_global_device_ids=true, to_apply=%add | all-reduce | flops 192 | bytes 1536
  44.7 11.0 %all_gather.59 = bf16[128,2048]{1,0:T(8,128)(2,1)S(1)} all-gather(bf16[128,512]{1,0:T(8,128)(2,1)} %param.16), channel_id=1, replica_groups=mesh['seq'=64,'head'=4] {'head'}, dimensions={1}, use_global_device_ids=true | all-gather | bytes 655360 | tf_op jit(solution)/shard_map/all_gather | solution.py:188
  59.4 40.8 %all-gather.11.cloned.1.call-done = bf16[256,128,128]{2,1,0:T(8,128)(2,1)} async-done(((bf16[4,128,128]{2,1,0:T(8,128)(2,1)}), bf16[256,128,128]{2,1,0:T(8,128)(2,1)}) %all-gather.11.cloned.1.call-update) | async-done | bytes 8388624 | tf_op jit(solution)/shard_map/all_gather | solution.py:15
  100.2 83.2 %all-gather.9.cloned.1.call-done = bf16[256,128,128]{2,1,0:T(8,128)(2,1)} async-done(((bf16[4,128,128]{2,1,0:T(8,128)(2,1)}), bf16[256,128,128]{2,1,0:T(8,128)(2,1)}) %all-gather.9.cloned.1.call-update) | async-done | bytes 8388624 | tf_op jit(solution)/shard_map/all_gather | solution.py:15
  183.3 323.7 %while.38 = (s32[]{:T(128)}, s32[]{:T(128)}, f32[4,128,128]{2,1,0:T(8,128)S(1)}, f32[4,128,128]{2,1,0:T(8,128)S(1)}, s32[]{:T(128)}, /*index=5*/s32[64]{0:T(128)...) while((s32[]{:T(128)}, s32[]{:T(128)}, ...), condition=%wide.region_1.2_spmd.clone, body=%wide.region_0.1_spmd.clone.sunk | while | flops 655373 | bytes 1310965 | solution.py:33
  508.1 1.4 fusion.25
  523.1 1.5 convolution_convert_fusion.1
  524.6 1.6 fusion.51
  527.1 1.6 fusion.30
  529.6 1.3 fusion.19
  530.9 1.3 convolution_convert_fusion
  532.4 1.4 fusion.36
  534.6 3.8 convolution_bitcast_fusion
  538.4 5.4 copy.169
  545.0 59.6 %all-gather.13.cloned.1.call-done = bf16[256,128,128]{2,1,0:T(8,128)(2,1)} async-done(((bf16[4,128,128]{2,1,0:T(8,128)(2,1)}), bf16[256,128,128]{2,1,0:T(8,128)(2,1)}) %all-gather.13.cloned.1.call-update) | async-done | bytes 8388624 | tf_op jit(solution)/shard_map/all_gather | solution.py:15
  604.6 83.0 %all-gather.15.cloned.1.call-done = bf16[256,128,128]{2,1,0:T(8,128)(2,1)} async-done(((bf16[4,128,128]{2,1,0:T(8,128)(2,1)}), bf16[256,128,128]{2,1,0:T(8,128)(2,1)}) %all-gather.15.cloned.1.call-update) | async-done | bytes 8388624 | tf_op jit(solution)/shard_map/all_gather | solution.py:15
  687.6 324.1 %while.39 = (s32[]{:T(128)}, s32[]{:T(128)}, f32[4,128,128]{2,1,0:T(8,128)S(1)}, f32[4,128,128]{2,1,0:T(8,128)S(1)}, s32[]{:T(128)}, /*index=5*/s32[64]{0:T(128)...) while((s32[]{:T(128)}, s32[]{:T(128)}, ...), condition=%wide.region_20.21_spmd.clone, body=%wide.region_19.20_spmd.clone.sunk | while | flops 655377 | bytes 1311027 | solution.py:33
  1012.1 1.3 fusion.21
  1015.0 1.3 fusion.8
  1016.4 1.4 fusion.7
  1017.8 1.3 fusion.20
  (537 shorter events, 341.1 us)
Async XLA Ops:
  7.2 50.3 %copy-start = (bf16[512,2048]{1,0:T(8,128)(2,1)S(1)}, bf16[512,2048]{1,0:T(8,128)(2,1)}, u32[]{:S(2)}) copy-start(bf16[512,2048]{1,0:T(8,128)(2,1)} %param.15) | copy-start | bytes 6291460
  7.2 93.0 %all-gather.11.cloned.1.call-start = ((), (), s32[]{:S(2)}) async-start(), calls=%async_computation.4 | async-start | bytes 8519680 | tf_op jit(solution)/shard_map/all_gather | solution.py:15
  12.8 170.5 %all-gather.9.cloned.1.call-start = ((), (), s32[]{:S(2)}) async-start(), calls=%async_computation.3 | async-start | bytes 8519680 | tf_op jit(solution)/shard_map/all_gather | solution.py:15
  15.7 588.8 %all-gather.13.cloned.1.call-start = ((), (), s32[]{:S(2)}) async-start(), calls=%async_computation.5 | async-start | bytes 8519680 | tf_op jit(solution)/shard_map/all_gather | solution.py:15
  56.5 464.2 %copy-start.2 = (f32[128,128]{1,0:T(8,128)}, f32[128,128]{1,0:T(8,128)S(1)}, u32[]{:S(2)}) copy-start(f32[128,128]{1,0:T(8,128)S(1)} %fusion.73) | copy-start | bytes 196612
  58.2 455.6 %copy-start.6 = (f32[128,512]{0,1:T(8,128)}, f32[128,512]{0,1:T(8,128)S(1)}, u32[]{:S(2)}) copy-start(f32[128,512]{0,1:T(8,128)S(1)} %fusion.90) | copy-start | bytes 786436
  58.2 448.8 %copy-start.23 = (s32[128]{0:T(128)S(1)}, s32[128]{0:T(128)}, u32[]{:S(2)}) copy-start(s32[128]{0:T(128)} %param.17) | copy-start | bytes 1540
  58.2 449.8 %copy-start.1 = (bf16[128,512]{1,0:T(8,128)(2,1)S(1)}, bf16[128,512]{1,0:T(8,128)(2,1)}, u32[]{:S(2)}) copy-start(bf16[128,512]{1,0:T(8,128)(2,1)} %param.12) | copy-start | bytes 393220
  58.2 449.8 %copy-start.17 = (f32[4]{0:T(128)S(1)}, f32[4]{0:T(128)}, u32[]{:S(2)}) copy-start(f32[4]{0:T(128)} %param.14) | copy-start | bytes 52
  507.1 5.2 copy-start.26
  507.6 15.4 %copy-start.25 = (f32[128]{0:T(128)}, f32[128]{0:T(128)S(1)}, u32[]{:S(2)}) copy-start(f32[128]{0:T(128)S(1)} %get-tuple-element.510) | copy-start | bytes 1540
  518.1 4.1 copy-start.18
  518.3 3.8 copy-start.20
  521.2 7.7 copy-start.3
  524.6 163.0 %all-gather.15.cloned.1.call-start = ((), (), s32[]{:S(2)}) async-start(), calls=%async_computation.6 | async-start | bytes 8519680 | tf_op jit(solution)/shard_map/all_gather | solution.py:15
  528.8 491.1 %reduce-scatter.5.cloned.1.call-start = ((), (), s32[]{:S(2)}) async-start(), calls=%async_computation.2 | async-start | bytes 655360 | tf_op jit(solution)/shard_map/reduce_scatter | solution.py:185
  532.3 487.6 %reduce-scatter.7.cloned.1.call-start = ((), (), s32[]{:S(2)}) async-start(), calls=%async_computation.7 | async-start | bytes 4259840
  538.4 5.4 copy-start.4
  538.4 5.4 copy-start.12
  543.8 143.8 %copy-start.27 = (s32[64]{0:T(128)S(1)}, s32[64]{0:T(128)}, u32[]{:S(2)}) copy-start(s32[64]{0:T(128)} %copy-done.26) | copy-start | bytes 772
  543.8 143.8 %copy-start.28 = (s32[64]{0:T(128)S(1)}, s32[64]{0:T(128)}, u32[]{:S(2)}) copy-start(s32[64]{0:T(128)} %get-tuple-element.685) | copy-start | bytes 772
  544.9 466.8 %copy-start.24 = (s32[128]{0:T(128)S(1)}, s32[128]{0:T(128)}, u32[]{:S(2)}) copy-start(s32[128]{0:T(128)} %param.17) | copy-start | bytes 1540
  545.0 467.2 %copy-start.8 = (f32[128,512]{0,1:T(8,128)S(1)}, f32[128,512]{0,1:T(8,128)}, u32[]{:S(2)}) copy-start(f32[128,512]{0,1:T(8,128)} %copy-done.6) | copy-start | bytes 786436
  687.6 326.6 %copy-start.15 = (bf16[128,512]{1,0:T(8,128)(2,1)S(1)}, bf16[128,512]{1,0:T(8,128)(2,1)}, u32[]{:S(2)}) copy-start(bf16[128,512]{1,0:T(8,128)(2,1)} %param.13) | copy-start | bytes 393220
  (11 other events, 24.5 us)
Sparse Core Ops, SparseCore 0:
  12.9 87.1 all-gather.10
  103.5 79.7 all-gather.8
  524.7 79.8 all-gather.12
  607.8 79.7 all-gather.14
  690.5 18.1 reduce-scatter.4
  713.3 141.4 reduce-scatter.6
where the time goes:
time: 1030 us
  loops' own time  339 us (33%)
  waiting for transfers between devices  267 us (26%)
  local copies, waits for them, and re-layouts  167 us (16%)
  other arithmetic  166 us (16%)
  matrix products  37.2 us (4%)
  blocking collectives  32.9 us (3%)
  between operations  17.3 us (2%)
    another operation x2, loops' own time, prefix(): return lax.fori_loop(0, devices, step, start)  339 us
    all_gather x4, waiting for transfers between devices, prefix(): lax.all_gather(part.astype(kind), axis)  267 us
    select_n x128, other arithmetic, step(): return jax.tree.map(lambda a, b: jnp.where(reached, a, b), new, before)  158 us
    dynamic_slice x256, local copies, waits for them, and re-layouts, step(): part[at].astype(own.dtype)  150 us
    dot_general x40, matrix products, matmul_high(): jnp.dot(left_side, right_side, precision=lax.Precision.HIGHEST, preferred...  27.7 us
    unnamed x1, blocking collectives  21.9 us
  transfers between devices with their start and end apart: 6, of which 4 were waited for; matrix products, arithmetic and copies ran while one was open for 19% of the time, Pallas kernels for 0%

commit v1 on v0

v1 whole, which is shorter than its diff:
```python
import functools

import jax
import jax.numpy as jnp
from jax import lax
from jax.experimental import pallas as pl
from jax.experimental.pallas import tpu as pltpu
from jax.sharding import PartitionSpec as P

CG_STEPS = 4
EPS = 1e-6
DH = 128
F32 = jnp.float32
BF = jnp.bfloat16
MESH = pl.DeviceIdType.MESH

SEQ_DIMS = (4, 8, 2)


def nn(a, b):
    return lax.dot_general(a, b, (((1,), (0,)), ((), ())), preferred_element_type=F32)


def nt(a, b):
    return lax.dot_general(a, b, (((1,), (1,)), ((), ())), preferred_element_type=F32)


def tn(a, b):
    return lax.dot_general(a, b, (((0,), (0,)), ((), ())), preferred_element_type=F32)


def halves(a):
    high = a.astype(BF)
    return high, (a - high.astype(F32)).astype(BF)


def kernel(
    dims, nx,
    ridge, q_in, k_in, v_in, w_in, og_in, doc_in,
    lay_out, gq_out, gk_out, gv_out, gw_out,
    q, k, v, w, doc, lab_own, lab,
    t_send, t_recv, p_send, p_recv, b_send, b_recv, r_send, r_recv,
    cot, cot_y, cot_t, mix, l_send, l_recv, l_own,
    gw_own, gw_send, gw_recv, z_send, z_recv,
    lay, gq, gk, gv, gw,
    load_sem, out_sem,
    lab_s, lab_r, t_s, t_r, p_s, p_r, b_s, b_r, r_s, r_r,
    cot_s, cot_r, coty_s, coty_r, mix_s, mix_r, l_s, l_r, gw_s, gw_r, z_s, z_r,
):
    ny, nz, nc = dims
    n = ny * nz * nc
    heads = ridge.shape[0]
    width = heads * DH
    me, mh = lax.axis_index("seq"), lax.axis_index("head")
    c = lax.rem(me, nc)
    z = lax.rem(me // nc, nz)
    y = me // (nc * nz)
    rows = t_send.shape[1]
    per_head = 2 * DH // rows

    def remote(src, dst, ssem, rsem, seq, head):
        return pltpu.make_async_remote_copy(
            src_ref=src, dst_ref=dst, send_sem=ssem, recv_sem=rsem,
            device_id=(seq, head), device_id_type=MESH,
        )

    def settle(ref, sem):
        pltpu.make_async_copy(ref, ref, sem).wait()

    loads = [
        pltpu.make_async_copy(src, dst, load_sem.at[i])
        for i, (src, dst) in enumerate(
            ((doc_in, doc), (k_in, k), (v_in, v), (og_in, cot.at[mh]), (w_in, w), (q_in, q))
        )
    ]
    for load in loads:
        load.start()

    barrier = pltpu.get_barrier_semaphore()

    @pl.loop(1, n)
    def _(i):
        pl.semaphore_signal(barrier, inc=1, device_id=(lax.rem(me + i, n), mh), device_id_type=MESH)

    for i in range(1, nx):
        pl.semaphore_signal(barrier, inc=1, device_id=(me, lax.rem(mh + i, nx)), device_id_type=MESH)

    loads[0].wait()
    doc_row = jnp.broadcast_to(doc[...].astype(F32), (DH, DH))
    doc_col = doc_row.T
    last, first = doc_col[DH - 1 : DH, :], doc_col[0:1, :]
    lab_own[0:1, :] = last
    lab_own[1:2, :] = first
    lab[me] = lab_own[...]
    below = lax.broadcasted_iota(jnp.int32, (DH, DH), 1) <= lax.broadcasted_iota(jnp.int32, (DH, DH), 0)
    same_doc = jnp.where((doc_row == doc_col) & below, 1.0, 0.0).astype(F32)
    tail = jnp.where(doc_col == last, 1.0, 0.0).astype(BF)
    head_rows = jnp.where(doc_col == first, 1.0, 0.0).astype(F32)

    loads[1].wait()
    loads[2].wait()
    for h in range(heads):
        cols = slice(h * DH, (h + 1) * DH)
        kh, vh = k[:, cols], v[:, cols]
        state = tn(jnp.concatenate([kh * tail, vh * tail], axis=1), kh).astype(BF)
        t_send[h * per_head : (h + 1) * per_head] = state.reshape(per_head, rows, DH)
    t_recv[me] = t_send[me]

    loads[3].wait()
    pl.semaphore_wait(barrier, n - 1 + nx - 1)

    def exchange(src, dst, ssem, rsem):
        @pl.loop(1, n)
        def _(i):
            to = lax.rem(me + i, n)
            remote(src.at[to], dst.at[me], ssem, rsem, to, mh).start()

    @pl.loop(1, n)
    def _(i):
        to = lax.rem(me + i, n)
        remote(lab_own, lab.at[me], lab_s, lab_r, to, mh).start()

    exchange(t_send, t_recv, t_s, t_r)
    for i in range(1, nx):
        remote(cot.at[mh], cot.at[mh], cot_s, cot_r, me, lax.rem(mh + i, nx)).start()

    loads[4].wait()
    settle(cot.at[pl.ds(0, nx - 1)], cot_r)
    for i in range(1, ny):
        to = lax.rem(y + i, ny)
        remote(cot.at[to], cot_y.at[y], coty_s, coty_r, (to * nz + z) * nc + c, mh).start()
    cot_y[y] = cot[y]
    do = nt(cot[0], w[:, 0:width])
    for b in range(1, nx):
        do = do + nt(cot[b], w[:, b * width : (b + 1) * width])

    do_high, do_low, score_two, target_own = [], [], [], []
    for h in range(heads):
        cols = slice(h * DH, (h + 1) * DH)
        kh, vh = k[:, cols], v[:, cols]
        high, low = halves(do[:, cols])
        two = (nt(high, vh) + nt(low, vh)) * same_doc
        two_high, two_low = halves(two)
        do_high.append(high)
        do_low.append(low)
        score_two.append(two)
        target_own.append(nn(two_high, kh) + nn(two_low, kh))

    def scan(src, dst, row, reverse):
        def step(i, carry):
            total, before = carry
            at = n - 1 - i if reverse else i
            dst[at] = total.astype(BF)
            label = lab[at, pl.ds(row, 1)]
            total = jnp.where(label == before, total, 0.0) + src[at].astype(F32)
            return total, label

        lax.fori_loop(
            0, n, step,
            (jnp.zeros((rows, DH), F32), jnp.full((1, DH), -1.0, F32)),
            unroll=4,
        )

    settle(lab.at[pl.ds(0, n - 1)], lab_r)
    settle(t_recv.at[pl.ds(0, n - 1)], t_r)
    scan(t_recv, p_send, 0, False)
    exchange(p_send, p_recv, p_s, p_r)
    p_recv[me] = p_send[me]

    label_in = jnp.where(me > 0, lab[jnp.maximum(me - 1, 0), pl.ds(0, 1)], -1.0)
    label_next = jnp.where(me < n - 1, lab[jnp.minimum(me + 1, n - 1), pl.ds(1, 1)], -1.0)
    carried = jnp.where(doc_col == label_in, 1.0, 0.0).astype(F32)
    later = jnp.where(doc_col == label_next, 1.0, 0.0).astype(F32)
    carried_two = jnp.concatenate([carried, carried], axis=0).astype(BF)
    same_two = jnp.concatenate([same_doc, same_doc], axis=0)

    settle(cot_y.at[pl.ds(0, ny - 1)], coty_r)
    strip = gw.shape[0]
    for b in range(ny):
        turned = cot_y[b].T
        for zz in range(nz):
            for cc in range(nc):
                at = (zz * nc + cc) * strip
                cot_t[cc, zz * strip : (zz + 1) * strip, b * DH : (b + 1) * DH] = turned[at : at + strip, :]

    loads[5].wait()
    settle(p_recv.at[pl.ds(0, n - 1)], p_r)

    keys, gram, x, r, p, rr = [], [], [], [], [], []
    for h in range(heads):
        cols = slice(h * DH, (h + 1) * DH)
        kh = k[:, cols]
        state = p_recv[h * per_head : (h + 1) * per_head].reshape(2 * DH, DH)
        value_in = state[DH:]
        target = carried * (nn(do_high[h], value_in) + nn(do_low[h], value_in)) + target_own[h]
        b = jnp.concatenate([q[:, cols].astype(F32), target], axis=0)
        keys.append(jnp.concatenate([kh, state[:DH]], axis=0))
        x.append(jnp.zeros_like(b))
        r.append(b)
        p.append(b)
        rr.append(jnp.sum(b * b, axis=1, keepdims=True))
    for number in range(CG_STEPS):
        for h in range(heads):
            cols = slice(h * DH, (h + 1) * DH)
            kh = k[:, cols]
            p_high, p_low = halves(p[h])
            scores = (nt(p_high, kh) + nt(p_low, kh)) * same_two
            s_high, s_low = halves(scores)
            applied = (
                nn(jnp.concatenate([s_high, p_high * carried_two], axis=1), keys[h])
                + nn(jnp.concatenate([s_low, p_low * carried_two], axis=1), keys[h])
                + ridge[h] * p[h]
            )
            step = rr[h] / (jnp.sum(p[h] * applied, axis=1, keepdims=True) + EPS)
            x[h] = x[h] + step * p[h]
            if number < CG_STEPS - 1:
                r[h] = r[h] - step * applied
                fresh = jnp.sum(r[h] * r[h], axis=1, keepdims=True)
                p[h] = r[h] + fresh / (rr[h] + EPS) * p[h]
                rr[h] = fresh

    x_high, x_low, score_x = [], [], []
    for h in range(heads):
        high, low = halves(x[h])
        x_high.append(high)
        x_low.append(low)
        rows_x = (head_rows * x[h][:DH]).astype(BF)
        both = tn(jnp.concatenate([do_high[h], high[DH:]], axis=1), rows_x)
        cross = both[DH:]
        state = jnp.concatenate([both[:DH], cross + cross.T], axis=0).astype(BF)
        b_send[h * per_head : (h + 1) * per_head] = state.reshape(per_head, rows, DH)
    exchange(b_send, b_recv, b_s, b_r)
    b_recv[me] = b_send[me]
    for h in range(heads):
        cols = slice(h * DH, (h + 1) * DH)
        kh, vh = k[:, cols], v[:, cols]
        value_in = p_recv[h * per_head : (h + 1) * per_head].reshape(2 * DH, DH)[DH:]
        scores = (nt(x_high[h], kh) + nt(x_low[h], kh)) * same_two
        score_x.append(scores)
        s_high, s_low = halves(scores[:DH])
        out = nn(s_high, vh) + nn(s_low, vh) + carried * (nt(x_high[h][:DH], value_in) + nt(x_low[h][:DH], value_in))
        mix[y, :, cols] = out.astype(BF)
        gq[:, cols] = x[h][DH:].astype(BF)
    pltpu.make_async_copy(gq, gq_out, out_sem.at[0]).start()
    for i in range(1, ny):
        to = lax.rem(y + i, ny)
        remote(mix.at[y], mix.at[y], mix_s, mix_r, (to * nz + z) * nc + c, mh).start()

    mixed = mix[y]
    for i in range(1, nx):
        to = lax.rem(mh + i, nx)
        part = nn(mixed, w[:, pl.ds(pl.multiple_of(to * width, width), width)])
        l_send[i] = part.astype(BF)
        remote(l_send.at[i], l_recv.at[mh], l_s, l_r, me, to).start()
    l_own[...] = nn(mixed, w[:, pl.ds(pl.multiple_of(mh * width, width), width)])
    l_recv[mh] = jnp.zeros((DH, width), BF)

    for h in range(heads):
        cols = slice(h * DH, (h + 1) * DH)
        one = score_x[h][:DH].astype(BF)
        rest = (score_two[h] - score_x[h][DH:]).astype(BF)
        gv[:, cols] = tn(one, do_high[h])
        gk[:, cols] = tn(rest, x_high[h][:DH]) - tn(one, x_high[h][DH:])

    settle(b_recv.at[pl.ds(0, n - 1)], b_r)
    scan(b_recv, r_send, 1, True)
    exchange(r_send, r_recv, r_s, r_r)
    r_recv[me] = r_send[me]

    settle(mix.at[pl.ds(0, ny - 1)], mix_r)
    gathered = mix[...].reshape(ny * DH, width)
    other = nc - 1 - c
    gw_send[...] = nn(cot_t[other], gathered).astype(BF).reshape(nz, strip, width)
    remote(gw_send, gw_recv, gw_s, gw_r, (y * nz + z) * nc + other, mh).start()
    gw_own[...] = nn(cot_t[c], gathered).reshape(nz, strip, width)
    settle(gw_recv, gw_r)
    z_send[...] = (gw_own[...] + gw_recv[...].astype(F32)).astype(BF)
    for i in range(1, nz):
        to = lax.rem(z + i, nz)
        remote(z_send.at[to], z_recv.at[z], z_s, z_r, (y * nz + to) * nc + c, mh).start()
    z_recv[z] = z_send[z]

    settle(l_recv.at[pl.ds(0, nx - 1)], l_r)
    total = l_own[...]
    for b in range(nx):
        total = total + l_recv[b].astype(F32)
    lay[...] = total.astype(BF)
    pltpu.make_async_copy(lay, lay_out, out_sem.at[1]).start()

    settle(r_recv.at[pl.ds(0, n - 1)], r_r)
    outs = [pltpu.make_async_copy(gq, gq_out, out_sem.at[0]), pltpu.make_async_copy(lay, lay_out, out_sem.at[1])]
    for h in range(heads):
        cols = slice(h * DH, (h + 1) * DH)
        kh, vh = k[:, cols], v[:, cols]
        state = r_recv[h * per_head : (h + 1) * per_head].reshape(2 * DH, DH)
        grad_state, gram_grad = state[:DH], state[DH:]
        q[:, cols] = (gv[:, cols] + later * nt(kh, grad_state)).astype(BF)
        k[:, cols] = (gk[:, cols] + later * (nn(vh, grad_state) - nn(kh, gram_grad))).astype(BF)
    outs += [pltpu.make_async_copy(q, gv_out, out_sem.at[2]), pltpu.make_async_copy(k, gk_out, out_sem.at[3])]
    outs[2].start()
    outs[3].start()

    settle(z_recv.at[pl.ds(0, nz - 1)], z_r)
    total = z_recv[0].astype(F32)
    for b in range(1, nz):
        total = total + z_recv[b].astype(F32)
    gw[...] = total
    outs.append(pltpu.make_async_copy(gw, gw_out, out_sem.at[4]))
    outs[4].start()

    settle(lab.at[pl.ds(0, n - 1)], lab_s)
    for src, sem in ((t_send, t_s), (p_send, p_s), (b_send, b_s), (r_send, r_s)):
        settle(src.at[pl.ds(0, n - 1)], sem)
    settle(cot.at[pl.ds(0, nx - 1)], cot_s)
    settle(cot_y.at[pl.ds(0, ny - 1)], coty_s)
    settle(mix.at[pl.ds(0, ny - 1)], mix_s)
    settle(l_send.at[pl.ds(1, nx - 1)], l_s)
    settle(gw_send, gw_s)
    settle(z_send.at[pl.ds(0, nz - 1)], z_s)
    for out in outs:
        out.wait()


def per_device(dims, nx, query_rows, key_rows, value_rows, ridge_reg, out_weight, out_grad, doc_ids):
    ny, nz, nc = dims
    n = ny * nz * nc
    heads = ridge_reg.shape[0]
    width = heads * DH
    rows = heads * 2 * DH // n
    strip = width // (nz * nc)
    states = [pltpu.VMEM((n, rows, DH), BF)] * 8
    dma = pltpu.SemaphoreType.DMA
    any_space = pl.BlockSpec(memory_space=pl.ANY)
    piece = jax.ShapeDtypeStruct((DH, width), BF)
    return pl.pallas_call(
        functools.partial(kernel, dims, nx),
        out_shape=(piece, piece, piece, piece, jax.ShapeDtypeStruct((strip, width), F32)),
        in_specs=[pl.BlockSpec(memory_space=pltpu.SMEM)] + [any_space] * 6,
        out_specs=(any_space,) * 5,
        scratch_shapes=[
            pltpu.VMEM((DH, width), BF),
            pltpu.VMEM((DH, width), BF),
            pltpu.VMEM((DH, width), BF),
            pltpu.VMEM((width, nx * width), BF),
            pltpu.VMEM((1, DH), jnp.int32),
            pltpu.VMEM((2, DH), F32),
            pltpu.VMEM((n, 2, DH), F32),
            *states,
            pltpu.VMEM((nx, DH, width), BF),
            pltpu.VMEM((ny, DH, width), BF),
            pltpu.VMEM((nc, nz * strip, ny * DH), BF),
            pltpu.VMEM((ny, DH, width), BF),
            pltpu.VMEM((nx, DH, width), BF),
            pltpu.VMEM((nx, DH, width), BF),
            pltpu.VMEM((DH, width), F32),
            pltpu.VMEM((nz, strip, width), F32),
            pltpu.VMEM((nz, strip, width), BF),
            pltpu.VMEM((nz, strip, width), BF),
            pltpu.VMEM((nz, strip, width), BF),
            pltpu.VMEM((nz, strip, width), BF),
            pltpu.VMEM((DH, width), BF),
            pltpu.VMEM((DH, width), BF),
            pltpu.VMEM((DH, width), F32),
            pltpu.VMEM((DH, width), F32),
            pltpu.VMEM((strip, width), F32),
            dma((6,)),
            dma((5,)),
        ]
        + [dma] * 22,
        compiler_params=pltpu.CompilerParams(collective_id=0, has_side_effects=True),
    )(ridge_reg, query_rows, key_rows, value_rows, out_weight, out_grad, doc_ids.reshape(1, -1))


def build(mesh, dims):
    nx = mesh.shape["head"]
    spec = P("seq", "head")
    return jax.shard_map(
        functools.partial(per_device, dims, nx),
        mesh=mesh,
        in_specs=(spec, spec, spec, P("head"), P("head", None), spec, P("seq")),
        out_specs=(spec,) * 5,
        check_vma=False,
    )


def solution(mesh):
    return build(mesh, SEQ_DIMS)
```

time: 1030 us -> 71.3 us (0.07)
  loops' own time: 339 us -> 0 us
  waiting for transfers between devices: 267 us -> 0 us
  other arithmetic: 166 us -> 0 us
  local copies, waits for them, and re-layouts: 167 us -> 7.74 us
  Pallas kernels: 0 us -> 62.7 us
  matrix products: 37.2 us -> 0 us
  blocking collectives: 32.9 us -> 0 us
  between operations: 17.3 us -> 0.64 us
    another operation x2 -> x0, loops' own time: 339 us -> none  [prefix(): return lax.fori_loop(0, devices, step, start)]
    all_gather x4 -> x0, waiting for transfers between devices: 267 us -> none  [prefix(): lax.all_gather(part.astype(kind), axis)]
    select_n x128 -> x0, other arithmetic: 158 us -> none  [step(): return jax.tree.map(lambda a, b: jnp.where(reached, a, b), new, before)]
    dynamic_slice x256 -> x0, local copies, waits for them, and re-layouts: 150 us -> none  [step(): part[at].astype(own.dtype)]
    pallas_call x0 -> x1, Pallas kernels: none -> 62.7 us  [per_device(): pl.pallas_call(functools.partial(kernel, dims, nx), out_shape=(piece, pie...]
    dot_general x44 -> x0, matrix products: 36.5 us -> none  [the longest x40 27.7 us: matmul_high(): jnp.dot(left_side, right_side, precision=lax.Precision.HIGHEST, preferred...]
    unnamed x1 -> x0, blocking collectives: 21.9 us -> none
    all_gather x1 -> x0, blocking collectives: 11 us -> none  [per_device(): cot_full = lax.all_gather(out_grad, 'head', axis=1, tiled=True)]
  transfers between devices with their start and end apart: 6 -> 0, of which waited for: 4 -> 0; matrix products, arithmetic and copies ran while one was open for 19% -> 0% of each run, Pallas kernels for 0% -> 0%
where the time goes in v1:
time: 71.3 us; the launch traced here: 71.1 us
  Pallas kernels  62.7 us (88%)
  local copies, waits for them, and re-layouts  7.74 us (11%)
    pallas_call x1, Pallas kernels, per_device(): pl.pallas_call(functools.partial(kernel, dims, nx), out_shape=(piece, pie...  62.7 us
    unnamed x5, local copies, waits for them, and re-layouts  7.74 us

profile of v1, /device:TPU:1, one launch (start us, length us, event | category | flops | bytes accessed | tf_op | source)
XLA Modules:
  0.0 71.1 jit_solution(1196567387674866030)
XLA Ops:
  0.6 62.7 %shard_map.110 = (bf16[128,512]{1,0:T(8,128)(2,1)}, bf16[128,512]{1,0:T(8,128)(2,1)}, bf16[128,512]{1,0:T(8,128)(2,1)}, bf16[128,512]{1,0:T(8,128)(2,1)}, f32[32,512]{1,0:T(8,128)}) custom-call(f32[4]{0:T(128)} %ridge.1, bf16[128,512]{1,0:T(8,128)(2,1)} %q_in.1, bf16[128,512]{1,0:T(8,128)(2,1)} %k_in.1, bf16[128,512]{1,0:T(8,128)(2,1)} %v_in.1, ...), custom_call_target="tpu_custom_call" | custom-call | tf_op jit(solution)/shard_map/pallas_call | solution.py:335
  63.4 1.6 %copy.17 = bf16[128,512]{1,0:T(8,128)(2,1)} copy(bf16[128,512]{1,0:T(8,128)(2,1)} %get-tuple-element.10) | data formatting | bytes 262144
  64.9 1.6 %copy.18 = bf16[128,512]{1,0:T(8,128)(2,1)} copy(bf16[128,512]{1,0:T(8,128)(2,1)} %get-tuple-element.11) | data formatting | bytes 262144
  66.5 1.6 %copy.19 = bf16[128,512]{1,0:T(8,128)(2,1)} copy(bf16[128,512]{1,0:T(8,128)(2,1)} %get-tuple-element.12) | data formatting | bytes 262144
  68.1 1.6 %copy.20 = bf16[128,512]{1,0:T(8,128)(2,1)} copy(bf16[128,512]{1,0:T(8,128)(2,1)} %get-tuple-element.13) | data formatting | bytes 262144
  69.6 1.5 %copy.21 = f32[32,512]{1,0:T(8,128)} copy(f32[32,512]{1,0:T(8,128)} %get-tuple-element.14) | data formatting | bytes 131072

commit v2 on v1

v2 whole, which is shorter than its diff:
```python
import functools

import jax
import jax.numpy as jnp
from jax import lax
from jax.experimental import pallas as pl
from jax.experimental.pallas import tpu as pltpu
from jax.sharding import PartitionSpec as P

CG_STEPS = 4
EPS = 1e-6
DH = 128
F32 = jnp.float32
BF = jnp.bfloat16
MESH = pl.DeviceIdType.MESH

SEQ_DIMS = (4, 8, 2)


def nn(a, b):
    return lax.dot_general(a, b, (((1,), (0,)), ((), ())), preferred_element_type=F32)


def nt(a, b):
    return lax.dot_general(a, b, (((1,), (1,)), ((), ())), preferred_element_type=F32)


def tn(a, b):
    return lax.dot_general(a, b, (((0,), (0,)), ((), ())), preferred_element_type=F32)


def halves(a):
    high = a.astype(BF)
    return high, (a - high.astype(F32)).astype(BF)


def kernel(
    dims, nx,
    ridge, q_in, k_in, v_in, w_in, og_in, doc_in,
    lay_out, gq_out, gk_out, gv_out, gw_out,
    q, k, v, w, doc, lab_own, lab_mate, lab_chip, lab, edge_own, edge,
    t_own, t_mate, t_send, t_recv, t_line, t_lines, p_send, p_recv, p_mate, p_all,
    b_own, b_mate, b_send, b_recv, b_line, b_lines, r_send, r_recv, r_mate, r_all,
    cot, cot_y, cot_t, mix, l_send, l_recv, l_own,
    gw_own, gw_send, gw_recv, z_send, z_recv,
    lay, gq, gk, gv, gw,
    load_sem, out_sem, send_sem, recv_sem,
):
    ny, nz, nc = dims
    heads = ridge.shape[0]
    width = heads * DH
    me, mh = lax.axis_index("seq"), lax.axis_index("head")
    c = lax.rem(me, nc)
    z = lax.rem(me // nc, nz)
    y = me // (nc * nz)
    other = nc - 1 - c
    rows = t_line.shape[0]
    strip = gw.shape[0]

    def at(yy, zz, cc):
        return (yy * nz + zz) * nc + cc

    mate = at(y, z, other)
    y_peers = [lax.rem(y + i, ny) for i in range(1, ny)]
    z_peers = [lax.rem(z + i, nz) for i in sorted(range(1, nz), key=lambda i: -min(i, nz - i))]
    x_peers = [lax.rem(mh + i, nx) for i in range(1, nx)]

    names = ("lab_mate", "lab", "edge", "t_mate", "t", "t_line", "p", "p_mate", "b_mate", "b", "b_line",
             "r", "r_mate", "cot", "cot_y", "mix", "l", "gw", "z")
    sems = {name: i for i, name in enumerate(names)}
    sent = []

    def send(name, src, dst, seq, head=None):
        copy = pltpu.make_async_remote_copy(
            src_ref=src, dst_ref=dst,
            send_sem=send_sem.at[sems[name]], recv_sem=recv_sem.at[sems[name]],
            device_id=(seq, mh if head is None else head), device_id_type=MESH,
        )
        copy.start()

    def settle(name, ref):
        sent.append((name, ref))
        pltpu.make_async_copy(ref, ref, recv_sem.at[sems[name]]).wait()

    loads = [
        pltpu.make_async_copy(src, dst, load_sem.at[i])
        for i, (src, dst) in enumerate(
            ((doc_in, doc), (k_in, k), (v_in, v), (og_in, cot.at[mh]), (w_in, w), (q_in, q))
        )
    ]
    for load in loads:
        load.start()

    barrier = pltpu.get_barrier_semaphore()
    peers = [(at(y, zz, c), mh) for zz in z_peers] + [(at(yy, z, c), mh) for yy in y_peers]
    peers += [(me, hh) for hh in x_peers] + [(mate, mh)]
    for peer in peers:
        pl.semaphore_signal(barrier, inc=1, device_id=peer, device_id_type=MESH)

    loads[0].wait()
    doc_row = jnp.broadcast_to(doc[...].astype(F32), (DH, DH))
    doc_col = doc_row.T
    last, first = doc_col[DH - 1 : DH, :], doc_col[0:1, :]
    lab_own[0:1, :] = last
    lab_own[1:2, :] = first
    below = lax.broadcasted_iota(jnp.int32, (DH, DH), 1) <= lax.broadcasted_iota(jnp.int32, (DH, DH), 0)
    same_doc = jnp.where((doc_row == doc_col) & below, 1.0, 0.0).astype(F32)
    tail = jnp.where(doc_col == last, 1.0, 0.0).astype(BF)
    head_rows = jnp.where(doc_col == first, 1.0, 0.0).astype(F32)

    in_half = heads // nc
    per_head = 2 * DH // rows

    def put_state(ref, h, state):
        first_slice = (h % in_half) * per_head
        ref[h // in_half, first_slice : first_slice + per_head] = state.astype(BF).reshape(per_head, rows, DH)

    def get_state(ref, h):
        first_slice = (h % in_half) * per_head
        return ref[h // in_half, first_slice : first_slice + per_head].reshape(2 * DH, DH)

    loads[1].wait()
    loads[2].wait()
    for h in range(heads):
        cols = slice(h * DH, (h + 1) * DH)
        kh, vh = k[:, cols], v[:, cols]
        put_state(t_own, h, tn(jnp.concatenate([kh * tail, vh * tail], axis=1), kh))

    loads[3].wait()
    pl.semaphore_wait(barrier, len(peers))

    def combine(own, from_mate, chip, row, leads):
        joined = jnp.where(lab_own[row : row + 1, :] == lab_mate[row : row + 1, :], 1.0, 0.0)
        own_part = jnp.where(leads, joined, 1.0)
        mate_part = jnp.where(leads, 1.0, joined)
        for i in range(nz):
            chip[i] = (own[c, i].astype(F32) * own_part + from_mate[i].astype(F32) * mate_part).astype(BF)

    def line_total(parts, line, row, reverse):
        total, before = jnp.zeros((rows, DH), F32), None
        for i in reversed(range(nz)) if reverse else range(nz):
            label = lab[i, row : row + 1, :]
            if before is not None:
                total = jnp.where(label == before, total, 0.0)
            total = total + parts[i].astype(F32)
            before = label
        line[...] = total.astype(BF)

    def incoming(lines, row, reverse):
        total, before = jnp.zeros((rows, DH), F32), jnp.full((1, DH), -1.0, F32)
        for i in reversed(range(ny)) if reverse else range(ny):
            label = edge[i, row : row + 1, :]
            grown = jnp.where(label == before, total, 0.0) + lines[i].astype(F32)
            reached = i > y if reverse else i < y
            total = jnp.where(reached, grown, total)
            before = jnp.where(reached, label, before)
        return total, before

    def scan(parts, total, before, out, row, reverse):
        chip_before = before
        for i in reversed(range(nz)) if reverse else range(nz):
            label = lab[i, row : row + 1, :]
            out[i] = total.astype(BF)
            chip_before = jnp.where(i == z, before, chip_before)
            total = jnp.where(label == before, total, 0.0) + parts[i].astype(F32)
            before = label
        return chip_before

    def spread(own, from_mate, chip, to_mate, whole, row, chip_before, leads):
        lead_label = jnp.where(leads, lab_own[row : row + 1, :], lab_mate[row : row + 1, :])
        joined = jnp.where(lead_label == chip_before, 1.0, 0.0)
        for i in range(nz):
            ahead = chip[i].astype(F32)
            lead_state = jnp.where(leads, own[c, i].astype(F32), from_mate[i].astype(F32))
            trail = lead_state + joined * ahead
            whole[c, i] = jnp.where(leads, ahead, trail).astype(BF)
            to_mate[i] = jnp.where(leads, trail, ahead).astype(BF)
        return jnp.where(leads, chip_before, lead_label)

    leads, leads_back = c == 0, c == nc - 1

    send("lab_mate", lab_own, lab_mate, mate)
    send("t_mate", t_own.at[other], t_mate, mate)
    for hh in x_peers:
        send("cot", cot.at[mh], cot.at[mh], me, hh)

    settle("lab_mate", lab_mate)
    lab_chip[0:1, :] = jnp.where(leads, lab_mate[0:1, :], lab_own[0:1, :])
    lab_chip[1:2, :] = jnp.where(leads, lab_own[1:2, :], lab_mate[1:2, :])
    lab[z] = lab_chip[...]
    for zz in z_peers:
        send("lab", lab_chip, lab.at[z], at(y, zz, c))
    settle("t_mate", t_mate)
    combine(t_own, t_mate, t_send, 0, leads)
    for zz in z_peers:
        send("t", t_send.at[zz], t_recv.at[z], at(y, zz, c))
    t_recv[z] = t_send[z]

    settle("lab", lab.at[pl.ds(0, nz - 1)])
    edge_own[0:1, :] = lab[nz - 1, 0:1, :]
    edge_own[1:2, :] = lab[0, 1:2, :]
    edge[y] = edge_own[...]
    for yy in y_peers:
        send("edge", edge_own, edge.at[y], at(yy, z, c))
    settle("t", t_recv.at[pl.ds(0, nz - 1)])
    line_total(t_recv, t_line, 0, False)
    for yy in y_peers:
        send("t_line", t_line, t_lines.at[y], at(yy, z, c))
    t_lines[y] = t_line[...]
    settle("edge", edge.at[pl.ds(0, ny - 1)])
    settle("t_line", t_lines.at[pl.ds(0, ny - 1)])
    total, before = incoming(t_lines, 0, False)
    chip_before = scan(t_recv, total, before, p_send, 0, False)
    for zz in z_peers:
        send("p", p_send.at[zz], p_recv.at[z], at(y, zz, c))
    p_recv[z] = p_send[z]

    loads[4].wait()
    settle("cot", cot.at[pl.ds(0, nx - 1)])
    for yy in y_peers:
        send("cot_y", cot.at[yy], cot_y.at[y], at(yy, z, c))
    cot_y[y] = cot[y]
    do = nt(cot[0], w[:, 0:width])
    for b in range(1, nx):
        do = do + nt(cot[b], w[:, b * width : (b + 1) * width])

    do_high, do_low, score_two, target_own = [], [], [], []
    for h in range(heads):
        cols = slice(h * DH, (h + 1) * DH)
        kh, vh = k[:, cols], v[:, cols]
        high, low = halves(do[:, cols])
        two = (nt(high, vh) + nt(low, vh)) * same_doc
        two_high, two_low = halves(two)
        do_high.append(high)
        do_low.append(low)
        score_two.append(two)
        target_own.append(nn(two_high, kh) + nn(two_low, kh))
    loads[5].wait()

    settle("p", p_recv.at[pl.ds(0, nz - 1)])
    label_in = spread(t_own, t_mate, p_recv, p_mate, p_all, 0, chip_before, leads)
    send("p_mate", p_mate, p_all.at[c], mate)
    carried = jnp.where(doc_col == label_in, 1.0, 0.0).astype(F32)
    carried_two = jnp.concatenate([carried, carried], axis=0).astype(BF)
    same_two = jnp.concatenate([same_doc, same_doc], axis=0)
    settle("p_mate", p_mate)

    keys, x, r, p, rr = [], [], [], [], []
    for h in range(heads):
        cols = slice(h * DH, (h + 1) * DH)
        kh = k[:, cols]
        state = get_state(p_all, h)
        value_in = state[DH:]
        target = carried * (nn(do_high[h], value_in) + nn(do_low[h], value_in)) + target_own[h]
        b = jnp.concatenate([q[:, cols].astype(F32), target], axis=0)
        keys.append(jnp.concatenate([kh, state[:DH]], axis=0))
        x.append(jnp.zeros_like(b))
        r.append(b)
        p.append(b)
        rr.append(jnp.sum(b * b, axis=1, keepdims=True))
    for number in range(CG_STEPS):
        for h in range(heads):
            cols = slice(h * DH, (h + 1) * DH)
            kh = k[:, cols]
            p_high, p_low = halves(p[h])
            scores = (nt(p_high, kh) + nt(p_low, kh)) * same_two
            s_high, s_low = halves(scores)
            applied = (
                nn(jnp.concatenate([s_high, p_high * carried_two], axis=1), keys[h])
                + nn(jnp.concatenate([s_low, p_low * carried_two], axis=1), keys[h])
                + ridge[h] * p[h]
            )
            step = rr[h] / (jnp.sum(p[h] * applied, axis=1, keepdims=True) + EPS)
            x[h] = x[h] + step * p[h]
            if number < CG_STEPS - 1:
                r[h] = r[h] - step * applied
                fresh = jnp.sum(r[h] * r[h], axis=1, keepdims=True)
                p[h] = r[h] + fresh / (rr[h] + EPS) * p[h]
                rr[h] = fresh

    x_high, x_low, score_x = [], [], []
    for h in range(heads):
        high, low = halves(x[h])
        x_high.append(high)
        x_low.append(low)
        rows_x = (head_rows * x[h][:DH]).astype(BF)
        both = tn(jnp.concatenate([do_high[h], high[DH:]], axis=1), rows_x)
        cross = both[DH:]
        put_state(b_own, h, jnp.concatenate([both[:DH], cross + cross.T], axis=0))
    send("b_mate", b_own.at[other], b_mate, mate)

    for h in range(heads):
        cols = slice(h * DH, (h + 1) * DH)
        kh, vh = k[:, cols], v[:, cols]
        value_in = get_state(p_all, h)[DH:]
        scores = (nt(x_high[h], kh) + nt(x_low[h], kh)) * same_two
        score_x.append(scores)
        s_high, s_low = halves(scores[:DH])
        out = nn(s_high, vh) + nn(s_low, vh) + carried * (nt(x_high[h][:DH], value_in) + nt(x_low[h][:DH], value_in))
        mix[y, :, cols] = out.astype(BF)
    for yy in y_peers:
        send("mix", mix.at[y], mix.at[y], at(yy, z, c))

    settle("b_mate", b_mate)
    combine(b_own, b_mate, b_send, 1, leads_back)
    for zz in z_peers:
        send("b", b_send.at[zz], b_recv.at[z], at(y, zz, c))
    b_recv[z] = b_send[z]

    for h in range(heads):
        gq[:, h * DH : (h + 1) * DH] = x[h][DH:].astype(BF)
    outs = [pltpu.make_async_copy(gq, gq_out, out_sem.at[0])]
    outs[0].start()
    mixed = mix[y]
    for i, hh in enumerate(x_peers):
        part = nn(mixed, w[:, pl.ds(pl.multiple_of(hh * width, width), width)])
        l_send[i] = part.astype(BF)
        send("l", l_send.at[i], l_recv.at[mh], me, hh)
    l_own[...] = nn(mixed, w[:, pl.ds(pl.multiple_of(mh * width, width), width)])
    l_recv[mh] = jnp.zeros((DH, width), BF)

    for h in range(heads):
        cols = slice(h * DH, (h + 1) * DH)
        one = score_x[h][:DH].astype(BF)
        rest = (score_two[h] - score_x[h][DH:]).astype(BF)
        gv[:, cols] = tn(one, do_high[h])
        gk[:, cols] = tn(rest, x_high[h][:DH]) - tn(one, x_high[h][DH:])

    settle("b", b_recv.at[pl.ds(0, nz - 1)])
    line_total(b_recv, b_line, 1, True)
    for yy in y_peers:
        send("b_line", b_line, b_lines.at[y], at(yy, z, c))
    b_lines[y] = b_line[...]

    settle("cot_y", cot_y.at[pl.ds(0, ny - 1)])
    for b in range(ny):
        turned = cot_y[b].T
        for zz in range(nz):
            for cc in range(nc):
                cut = (zz * nc + cc) * strip
                cot_t[cc, zz * strip : (zz + 1) * strip, b * DH : (b + 1) * DH] = turned[cut : cut + strip, :]

    settle("b_line", b_lines.at[pl.ds(0, ny - 1)])
    total, before = incoming(b_lines, 1, True)
    chip_before = scan(b_recv, total, before, r_send, 1, True)
    for zz in z_peers:
        send("r", r_send.at[zz], r_recv.at[z], at(y, zz, c))
    r_recv[z] = r_send[z]

    settle("mix", mix.at[pl.ds(0, ny - 1)])
    gathered = mix[...].reshape(ny * DH, width)
    gw_send[...] = nn(cot_t[other], gathered).astype(BF).reshape(nz, strip, width)
    send("gw", gw_send, gw_recv, mate)
    gw_own[...] = nn(cot_t[c], gathered).reshape(nz, strip, width)
    settle("gw", gw_recv)
    z_send[...] = (gw_own[...] + gw_recv[...].astype(F32)).astype(BF)
    for zz in z_peers:
        send("z", z_send.at[zz], z_recv.at[z], at(y, zz, c))
    z_recv[z] = z_send[z]

    settle("l", l_recv.at[pl.ds(0, nx - 1)])
    total = l_own[...]
    for b in range(nx):
        total = total + l_recv[b].astype(F32)
    lay[...] = total.astype(BF)
    outs.append(pltpu.make_async_copy(lay, lay_out, out_sem.at[1]))
    outs[1].start()

    settle("r", r_recv.at[pl.ds(0, nz - 1)])
    label_next = spread(b_own, b_mate, r_recv, r_mate, r_all, 1, chip_before, leads_back)
    send("r_mate", r_mate, r_all.at[c], mate)
    later = jnp.where(doc_col == label_next, 1.0, 0.0).astype(F32)
    settle("r_mate", r_mate)
    for h in range(heads):
        cols = slice(h * DH, (h + 1) * DH)
        kh, vh = k[:, cols], v[:, cols]
        state = get_state(r_all, h)
        grad_state, gram_grad = state[:DH], state[DH:]
        q[:, cols] = (gv[:, cols] + later * nt(kh, grad_state)).astype(BF)
        k[:, cols] = (gk[:, cols] + later * (nn(vh, grad_state) - nn(kh, gram_grad))).astype(BF)
    outs += [pltpu.make_async_copy(q, gv_out, out_sem.at[2]), pltpu.make_async_copy(k, gk_out, out_sem.at[3])]
    outs[2].start()
    outs[3].start()

    settle("z", z_recv.at[pl.ds(0, nz - 1)])
    total = z_recv[0].astype(F32)
    for b in range(1, nz):
        total = total + z_recv[b].astype(F32)
    gw[...] = total
    outs.append(pltpu.make_async_copy(gw, gw_out, out_sem.at[4]))
    outs[4].start()

    for name, ref in sent:
        pltpu.make_async_copy(ref, ref, send_sem.at[sems[name]]).wait()
    for out in outs:
        out.wait()


def move(*refs):
    count = (len(refs) - 1) // 3
    ins, outs, held, sem = refs[:count], refs[count : 2 * count], refs[2 * count : 3 * count], refs[-1]
    reads = [pltpu.make_async_copy(a, b, sem.at[0, i]) for i, (a, b) in enumerate(zip(ins, held))]
    writes = [pltpu.make_async_copy(a, b, sem.at[1, i]) for i, (a, b) in enumerate(zip(held, outs))]
    for read in reads:
        read.start()
    for read, write in zip(reads, writes):
        read.wait()
        write.start()
    for write in writes:
        write.wait()


def per_device(dims, nx, query_rows, key_rows, value_rows, ridge_reg, out_weight, out_grad, doc_ids):
    ny, nz, nc = dims
    heads = ridge_reg.shape[0]
    width = heads * DH
    rows = heads * 2 * DH // (nc * nz)
    strip = width // (nz * nc)
    any_space = pl.BlockSpec(memory_space=pl.ANY)
    piece = jax.ShapeDtypeStruct((DH, width), BF)
    half = pltpu.VMEM((nz, rows, DH), BF)
    both = pltpu.VMEM((nc, nz, rows, DH), BF)
    line = pltpu.VMEM((rows, DH), BF)
    lines = pltpu.VMEM((ny, rows, DH), BF)
    label = pltpu.VMEM((2, DH), F32)
    wide = pltpu.VMEM((DH, width), BF)
    results = (piece, piece, piece, piece, jax.ShapeDtypeStruct((strip, width), F32))
    states = [both, half, half, half, line, lines, half, half, half, both]
    made = pl.pallas_call(
        functools.partial(kernel, dims, nx),
        out_shape=results,
        in_specs=[pl.BlockSpec(memory_space=pltpu.SMEM)] + [any_space] * 6,
        out_specs=(any_space,) * 5,
        scratch_shapes=[
            wide,
            wide,
            wide,
            pltpu.VMEM((width, nx * width), BF),
            pltpu.VMEM((1, DH), jnp.int32),
            label,
            label,
            label,
            pltpu.VMEM((nz, 2, DH), F32),
            label,
            pltpu.VMEM((ny, 2, DH), F32),
            *states,
            *states,
            pltpu.VMEM((nx, DH, width), BF),
            pltpu.VMEM((ny, DH, width), BF),
            pltpu.VMEM((nc, nz * strip, ny * DH), BF),
            pltpu.VMEM((ny, DH, width), BF),
            pltpu.VMEM((nx, DH, width), BF),
            pltpu.VMEM((nx, DH, width), BF),
            pltpu.VMEM((DH, width), F32),
            pltpu.VMEM((nz, strip, width), F32),
            pltpu.VMEM((nz, strip, width), BF),
            pltpu.VMEM((nz, strip, width), BF),
            pltpu.VMEM((nz, strip, width), BF),
            pltpu.VMEM((nz, strip, width), BF),
            wide,
            wide,
            pltpu.VMEM((DH, width), F32),
            pltpu.VMEM((DH, width), F32),
            pltpu.VMEM((strip, width), F32),
            pltpu.SemaphoreType.DMA((6,)),
            pltpu.SemaphoreType.DMA((5,)),
            pltpu.SemaphoreType.DMA((19,)),
            pltpu.SemaphoreType.DMA((19,)),
        ],
        compiler_params=pltpu.CompilerParams(collective_id=0, has_side_effects=True),
    )(ridge_reg, query_rows, key_rows, value_rows, out_weight, out_grad, doc_ids.reshape(1, -1))
    return pl.pallas_call(
        move,
        out_shape=results,
        in_specs=[any_space] * 5,
        out_specs=(any_space,) * 5,
        scratch_shapes=[wide] * 4 + [pltpu.VMEM((strip, width), F32), pltpu.SemaphoreType.DMA((2, 5))],
    )(*made)


def build(mesh, dims):
    nx = mesh.shape["head"]
    spec = P("seq", "head")
    return jax.shard_map(
        functools.partial(per_device, dims, nx),
        mesh=mesh,
        in_specs=(spec, spec, spec, P("head"), P("head", None), spec, P("seq")),
        out_specs=(spec,) * 5,
        check_vma=False,
    )


def solution(mesh):
    return build(mesh, SEQ_DIMS)
```

time: 71.3 us -> 55.7 us (0.78)
  Pallas kernels: 62.7 us -> 54.9 us
  local copies, waits for them, and re-layouts: 7.74 us -> 0 us
    pallas_call x1 -> x2, Pallas kernels: 62.7 us -> 54.9 us  [the longest x1 53.1 us: per_device(): pl.pallas_call(functools.partial(kernel, dims, nx), out_shape=results, in...]
    unnamed x5 -> x0, local copies, waits for them, and re-layouts: 7.74 us -> none
where the time goes in v2:
time: 55.7 us; the launch traced here: 55.6 us
  Pallas kernels  54.9 us (99%)
  between operations  0.64 us (1%)
    pallas_call x1, Pallas kernels, per_device(): pl.pallas_call(functools.partial(kernel, dims, nx), out_shape=results, in...  53.1 us
    pallas_call x1, Pallas kernels, per_device(): pl.pallas_call(move, out_shape=results, in_specs=[any_space] * 5, out_spe...  1.85 us

profile of v2, /device:TPU:1, one launch (start us, length us, event | category | flops | bytes accessed | tf_op | source)
XLA Modules:
  0.0 55.6 jit_solution(1933479553499882353)
XLA Ops:
  0.6 53.1 %shard_map.110 = (bf16[128,512]{1,0:T(8,128)(2,1)}, bf16[128,512]{1,0:T(8,128)(2,1)}, bf16[128,512]{1,0:T(8,128)(2,1)}, bf16[128,512]{1,0:T(8,128)(2,1)}, f32[32,512]{1,0:T(8,128)}) custom-call(f32[4]{0:T(128)} %ridge.1, bf16[128,512]{1,0:T(8,128)(2,1)} %q_in.1, bf16[128,512]{1,0:T(8,128)(2,1)} %k_in.1, bf16[128,512]{1,0:T(8,128)(2,1)} %v_in.1, ...), custom_call_target="tpu_custom_call" | custom-call | tf_op jit(solution)/shard_map/pallas_call | solution.py:429
  53.7 1.9 %shard_map.111 = (bf16[128,512]{1,0:T(8,128)(2,1)}, bf16[128,512]{1,0:T(8,128)(2,1)}, bf16[128,512]{1,0:T(8,128)(2,1)}, bf16[128,512]{1,0:T(8,128)(2,1)}, f32[32,512]{1,0:T(8,128)}) custom-call(bf16[128,512]{1,0:T(8,128)(2,1)} %get-tuple-element.10.refs_0_, bf16[128,512]{1,0:T(8,128)(2,1)} %get-tuple-element.11.refs_1_, ...), custom_call_target="tpu_custom_call" | custom-call | tf_op jit(solution)/shard_map/pallas_call | solution.py:472

commit v3 on v2

--- a/solution.py
+++ b/solution.py
@@ -36,18 +36,19 @@
 
 def kernel(
     dims, nx,
-    ridge, q_in, k_in, v_in, w_in, og_in, doc_in,
-    lay_out, gq_out, gk_out, gv_out, gw_out,
+    ridge_in, q_in, k_in, v_in, w_in, og_in, doc_in,
+    lay, gq, gk_out, gv_out, gw,
+    ridge,
     q, k, v, w, doc, lab_own, lab_mate, lab_chip, lab, edge_own, edge,
     t_own, t_mate, t_send, t_recv, t_line, t_lines, p_send, p_recv, p_mate, p_all,
     b_own, b_mate, b_send, b_recv, b_line, b_lines, r_send, r_recv, r_mate, r_all,
     cot, cot_y, cot_t, mix, l_send, l_recv, l_own,
     gw_own, gw_send, gw_recv, z_send, z_recv,
-    lay, gq, gk, gv, gw,
-    load_sem, out_sem, send_sem, recv_sem,
+    gk, gv,
+    load_sem, send_sem, recv_sem,
 ):
     ny, nz, nc = dims
-    heads = ridge.shape[0]
+    heads = ridge.shape[1]
     width = heads * DH
     me, mh = lax.axis_index("seq"), lax.axis_index("head")
     c = lax.rem(me, nc)
@@ -85,7 +86,7 @@
     loads = [
         pltpu.make_async_copy(src, dst, load_sem.at[i])
         for i, (src, dst) in enumerate(
-            ((doc_in, doc), (k_in, k), (v_in, v), (og_in, cot.at[mh]), (w_in, w), (q_in, q))
+            ((doc_in, doc), (k_in, k), (v_in, v), (og_in, cot.at[mh]), (w_in, w), (q_in, q), (ridge_in, ridge))
         )
     ]
     for load in loads:
@@ -236,6 +237,7 @@
         score_two.append(two)
         target_own.append(nn(two_high, kh) + nn(two_low, kh))
     loads[5].wait()
+    loads[6].wait()
 
     settle("p", p_recv.at[pl.ds(0, nz - 1)])
     label_in = spread(t_own, t_mate, p_recv, p_mate, p_all, 0, chip_before, leads)
@@ -268,7 +270,7 @@
             applied = (
                 nn(jnp.concatenate([s_high, p_high * carried_two], axis=1), keys[h])
                 + nn(jnp.concatenate([s_low, p_low * carried_two], axis=1), keys[h])
-                + ridge[h] * p[h]
+                + ridge[0, h] * p[h]
             )
             step = rr[h] / (jnp.sum(p[h] * applied, axis=1, keepdims=True) + EPS)
             x[h] = x[h] + step * p[h]
@@ -309,8 +311,6 @@
 
     for h in range(heads):
         gq[:, h * DH : (h + 1) * DH] = x[h][DH:].astype(BF)
-    outs = [pltpu.make_async_copy(gq, gq_out, out_sem.at[0])]
-    outs[0].start()
     mixed = mix[y]
     for i, hh in enumerate(x_peers):
         part = nn(mixed, w[:, pl.ds(pl.multiple_of(hh * width, width), width)])
@@ -340,18 +340,18 @@
                 cut = (zz * nc + cc) * strip
                 cot_t[cc, zz * strip : (zz + 1) * strip, b * DH : (b + 1) * DH] = turned[cut : cut + strip, :]
 
-    settle("b_line", b_lines.at[pl.ds(0, ny - 1)])
-    total, before = incoming(b_lines, 1, True)
-    chip_before = scan(b_recv, total, before, r_send, 1, True)
-    for zz in z_peers:
-        send("r", r_send.at[zz], r_recv.at[z], at(y, zz, c))
-    r_recv[z] = r_send[z]
-
     settle("mix", mix.at[pl.ds(0, ny - 1)])
     gathered = mix[...].reshape(ny * DH, width)
     gw_send[...] = nn(cot_t[other], gathered).astype(BF).reshape(nz, strip, width)
     send("gw", gw_send, gw_recv, mate)
     gw_own[...] = nn(cot_t[c], gathered).reshape(nz, strip, width)
+    settle("b_line", b_lines.at[pl.ds(0, ny - 1)])
+    total, before = incoming(b_lines, 1, True)
+    chip_before = scan(b_recv, total, before, r_send, 1, True)
+    for zz in z_peers:
+        send("r", r_send.at[zz], r_recv.at[z], at(y, zz, c))
+    r_recv[z] = r_send[z]
+
     settle("gw", gw_recv)
     z_send[...] = (gw_own[...] + gw_recv[...].astype(F32)).astype(BF)
     for zz in z_peers:
@@ -363,8 +363,6 @@
     for b in range(nx):
         total = total + l_recv[b].astype(F32)
     lay[...] = total.astype(BF)
-    outs.append(pltpu.make_async_copy(lay, lay_out, out_sem.at[1]))
-    outs[1].start()
 
     settle("r", r_recv.at[pl.ds(0, nz - 1)])
     label_next = spread(b_own, b_mate, r_recv, r_mate, r_all, 1, chip_before, leads_back)
@@ -376,35 +374,24 @@
         kh, vh = k[:, cols], v[:, cols]
         state = get_state(r_all, h)
         grad_state, gram_grad = state[:DH], state[DH:]
-        q[:, cols] = (gv[:, cols] + later * nt(kh, grad_state)).astype(BF)
-        k[:, cols] = (gk[:, cols] + later * (nn(vh, grad_state) - nn(kh, gram_grad))).astype(BF)
-    outs += [pltpu.make_async_copy(q, gv_out, out_sem.at[2]), pltpu.make_async_copy(k, gk_out, out_sem.at[3])]
-    outs[2].start()
-    outs[3].start()
+        gv_out[:, cols] = (gv[:, cols] + later * nt(kh, grad_state)).astype(BF)
+        gk_out[:, cols] = (gk[:, cols] + later * (nn(vh, grad_state) - nn(kh, gram_grad))).astype(BF)
 
     settle("z", z_recv.at[pl.ds(0, nz - 1)])
     total = z_recv[0].astype(F32)
     for b in range(1, nz):
         total = total + z_recv[b].astype(F32)
     gw[...] = total
-    outs.append(pltpu.make_async_copy(gw, gw_out, out_sem.at[4]))
-    outs[4].start()
 
     for name, ref in sent:
         pltpu.make_async_copy(ref, ref, send_sem.at[sems[name]]).wait()
-    for out in outs:
-        out.wait()
 
 
 def move(*refs):
-    count = (len(refs) - 1) // 3
-    ins, outs, held, sem = refs[:count], refs[count : 2 * count], refs[2 * count : 3 * count], refs[-1]
-    reads = [pltpu.make_async_copy(a, b, sem.at[0, i]) for i, (a, b) in enumerate(zip(ins, held))]
-    writes = [pltpu.make_async_copy(a, b, sem.at[1, i]) for i, (a, b) in enumerate(zip(held, outs))]
-    for read in reads:
-        read.start()
-    for read, write in zip(reads, writes):
-        read.wait()
+    count = (len(refs) - 1) // 2
+    ins, outs, sem = refs[:count], refs[count : 2 * count], refs[-1]
+    writes = [pltpu.make_async_copy(a, b, sem.at[i]) for i, (a, b) in enumerate(zip(ins, outs))]
+    for write in writes:
         write.start()
     for write in writes:
         write.wait()
@@ -417,21 +404,21 @@
     rows = heads * 2 * DH // (nc * nz)
     strip = width // (nz * nc)
     any_space = pl.BlockSpec(memory_space=pl.ANY)
-    piece = jax.ShapeDtypeStruct((DH, width), BF)
     half = pltpu.VMEM((nz, rows, DH), BF)
     both = pltpu.VMEM((nc, nz, rows, DH), BF)
     line = pltpu.VMEM((rows, DH), BF)
     lines = pltpu.VMEM((ny, rows, DH), BF)
     label = pltpu.VMEM((2, DH), F32)
     wide = pltpu.VMEM((DH, width), BF)
-    results = (piece, piece, piece, piece, jax.ShapeDtypeStruct((strip, width), F32))
+    held = (wide, wide, wide, wide, pltpu.VMEM((strip, width), F32))
     states = [both, half, half, half, line, lines, half, half, half, both]
     made = pl.pallas_call(
         functools.partial(kernel, dims, nx),
-        out_shape=results,
-        in_specs=[pl.BlockSpec(memory_space=pltpu.SMEM)] + [any_space] * 6,
-        out_specs=(any_space,) * 5,
+        out_shape=held,
+        in_specs=[any_space] * 7,
+        out_specs=(pl.BlockSpec(memory_space=pltpu.VMEM),) * 5,
         scratch_shapes=[
+            pltpu.SMEM((1, heads), F32),
             wide,
             wide,
             wide,
@@ -457,25 +444,21 @@
             pltpu.VMEM((nz, strip, width), BF),
             pltpu.VMEM((nz, strip, width), BF),
             pltpu.VMEM((nz, strip, width), BF),
-            wide,
-            wide,
             pltpu.VMEM((DH, width), F32),
             pltpu.VMEM((DH, width), F32),
-            pltpu.VMEM((strip, width), F32),
-            pltpu.SemaphoreType.DMA((6,)),
-            pltpu.SemaphoreType.DMA((5,)),
+            pltpu.SemaphoreType.DMA((7,)),
             pltpu.SemaphoreType.DMA((19,)),
             pltpu.SemaphoreType.DMA((19,)),
         ],
         compiler_params=pltpu.CompilerParams(collective_id=0, has_side_effects=True),
-    )(ridge_reg, query_rows, key_rows, value_rows, out_weight, out_grad, doc_ids.reshape(1, -1))
+    )(ridge_reg.reshape(1, -1), query_rows, key_rows, value_rows, out_weight, out_grad, doc_ids.reshape(1, -1))
     return pl.pallas_call(
         move,
-        out_shape=results,
-        in_specs=[any_space] * 5,
-        out_specs=(any_space,) * 5,
-        scratch_shapes=[wide] * 4 + [pltpu.VMEM((strip, width), F32), pltpu.SemaphoreType.DMA((2, 5))],
-    )(*made)
+        out_shape=[jax.ShapeDtypeStruct(a.shape, a.dtype) for a in made],
+        in_specs=[pl.BlockSpec(memory_space=pltpu.VMEM)] * 5,
+        out_specs=[any_space] * 5,
+        scratch_shapes=[pltpu.SemaphoreType.DMA((5,))],
+    )(*[pltpu.with_memory_space_constraint(a, pltpu.VMEM) for a in made])
 
 
 def build(mesh, dims):

time: 55.7 us -> 51.7 us (0.928)
  Pallas kernels: 54.9 us -> 50.8 us
    pallas_call x2, Pallas kernels: 54.9 us -> 50.8 us  [the longest x1 49.9 us: per_device(): pl.pallas_call(functools.partial(kernel, dims, nx), out_shape=held, in_sp...]
where the time goes in v3:
time: 51.7 us; the launch traced here: 51.4 us
  Pallas kernels  50.8 us (98%)
  between operations  0.64 us (1%)
    pallas_call x1, Pallas kernels, per_device(): pl.pallas_call(functools.partial(kernel, dims, nx), out_shape=held, in_sp...  49.9 us

profile of v3, /device:TPU:1, one launch (start us, length us, event | category | flops | bytes accessed | tf_op | source)
XLA Modules:
  0.0 51.4 jit_solution(10507198018642420348)
XLA Ops:
  0.6 49.9 %shard_map.110 = (bf16[128,512]{1,0:T(8,128)(2,1)S(1)}, bf16[128,512]{1,0:T(8,128)(2,1)S(1)}, bf16[128,512]{1,0:T(8,128)(2,1)S(1)}, bf16[128,512]{1,0:T(8,128)(2,1)S(1)}, f32[32,512]{1,0:T(8,128)S(1)}) custom-call(f32[1,4]{1,0:T(1,128)} %bitcast.2, bf16[128,512]{1,0:T(8,128)(2,1)} %q_in.1, bf16[128,512]{1,0:T(8,128)(2,1)} %k_in.1, bf16[128,512]{1,0:T(8,128)(2,1)} %v_in.1, ...), custom_call_target="tpu_custom_call" | custom-call | tf_op jit(solution)/shard_map/pallas_call | solution.py:415
  50.6 0.8 %shard_map.111 = (bf16[128,512]{1,0:T(8,128)(2,1)}, bf16[128,512]{1,0:T(8,128)(2,1)}, bf16[128,512]{1,0:T(8,128)(2,1)}, bf16[128,512]{1,0:T(8,128)(2,1)}, f32[32,512]{1,0:T(8,128)}) custom-call(bf16[128,512]{1,0:T(8,128)(2,1)S(1)} %get-tuple-element.10.refs_0_, bf16[128,512]{1,0:T(8,128)(2,1)S(1)} %get-tuple-element.11.refs_1_, ...), custom_call_target="tpu_custom_call" | custom-call | tf_op jit(solution)/shard_map/pallas_call | solution.py:455

commit v4 on v3

--- a/solution.py
+++ b/solution.py
@@ -32,6 +32,11 @@
 def halves(a):
     high = a.astype(BF)
     return high, (a - high.astype(F32)).astype(BF)
+
+
+def twice(product, high, low, right):
+    axis = 1 if product is nt else 0
+    return product(jnp.concatenate([high, low], axis=1), jnp.concatenate([right, right], axis=axis))
 
 
 def kernel(
@@ -42,7 +47,7 @@
     q, k, v, w, doc, lab_own, lab_mate, lab_chip, lab, edge_own, edge,
     t_own, t_mate, t_send, t_recv, t_line, t_lines, p_send, p_recv, p_mate, p_all,
     b_own, b_mate, b_send, b_recv, b_line, b_lines, r_send, r_recv, r_mate, r_all,
-    cot, cot_y, cot_t, mix, l_send, l_recv, l_own,
+    cot, cot_y, cot_t, do_all, target_own, x_all, mix, l_send, l_recv, l_own,
     gw_own, gw_send, gw_recv, z_send, z_recv,
     gk, gv,
     load_sem, send_sem, recv_sem,
@@ -62,12 +67,12 @@
         return (yy * nz + zz) * nc + cc
 
     mate = at(y, z, other)
-    y_peers = [lax.rem(y + i, ny) for i in range(1, ny)]
+    y_peers = [lax.rem(y + i, ny) for i in sorted(range(1, ny), key=lambda i: -min(i, ny - i))]
     z_peers = [lax.rem(z + i, nz) for i in sorted(range(1, nz), key=lambda i: -min(i, nz - i))]
     x_peers = [lax.rem(mh + i, nx) for i in range(1, nx)]
 
     names = ("lab_mate", "lab", "edge", "t_mate", "t", "t_line", "p", "p_mate", "b_mate", "b", "b_line",
-             "r", "r_mate", "cot", "cot_y", "mix", "l", "gw", "z")
+             "r", "r_mate", "cot", "cot_y", "l", "mix0", "mix1", "gw0", "gw1", "z0", "z1")
     sems = {name: i for i, name in enumerate(names)}
     sent = []
 
@@ -111,22 +116,28 @@
 
     in_half = heads // nc
     per_head = 2 * DH // rows
-
-    def put_state(ref, h, state):
-        first_slice = (h % in_half) * per_head
-        ref[h // in_half, first_slice : first_slice + per_head] = state.astype(BF).reshape(per_head, rows, DH)
-
-    def get_state(ref, h):
-        first_slice = (h % in_half) * per_head
-        return ref[h // in_half, first_slice : first_slice + per_head].reshape(2 * DH, DH)
+    chunk = in_half * DH
+    order = [(half, i) for half in range(nc) for i in range(in_half)]
+
+    def put_state(ref, half, i, state):
+        ref[half, i * per_head : (i + 1) * per_head] = state.astype(BF).reshape(per_head, rows, DH)
+
+    def get_state(ref, half, i):
+        return ref[half, i * per_head : (i + 1) * per_head].reshape(2 * DH, DH)
+
+    def cols_of(half, i):
+        start = (half * in_half + i) * DH
+        return pl.ds(start if isinstance(start, int) else pl.multiple_of(start, DH), DH)
 
     loads[1].wait()
     loads[2].wait()
-    for h in range(heads):
-        cols = slice(h * DH, (h + 1) * DH)
-        kh, vh = k[:, cols], v[:, cols]
-        put_state(t_own, h, tn(jnp.concatenate([kh * tail, vh * tail], axis=1), kh))
-
+    def gram(half):
+        for i in range(in_half):
+            cols = cols_of(half, i)
+            kh, vh = k[:, cols], v[:, cols]
+            put_state(t_own, half, i, tn(jnp.concatenate([kh * tail, vh * tail], axis=1), kh))
+
+    gram(other)
     loads[3].wait()
     pl.semaphore_wait(barrier, len(peers))
 
@@ -184,6 +195,7 @@
     send("t_mate", t_own.at[other], t_mate, mate)
     for hh in x_peers:
         send("cot", cot.at[mh], cot.at[mh], me, hh)
+    gram(c)
 
     settle("lab_mate", lab_mate)
     lab_chip[0:1, :] = jnp.where(leads, lab_mate[0:1, :], lab_own[0:1, :])
@@ -224,18 +236,17 @@
     do = nt(cot[0], w[:, 0:width])
     for b in range(1, nx):
         do = do + nt(cot[b], w[:, b * width : (b + 1) * width])
-
-    do_high, do_low, score_two, target_own = [], [], [], []
-    for h in range(heads):
-        cols = slice(h * DH, (h + 1) * DH)
+    do_all[...] = do
+
+    do_high, score_two = [], []
+    for h, (half, i) in enumerate(order):
+        cols = cols_of(half, i)
         kh, vh = k[:, cols], v[:, cols]
-        high, low = halves(do[:, cols])
-        two = (nt(high, vh) + nt(low, vh)) * same_doc
-        two_high, two_low = halves(two)
+        high, low = halves(do[:, h * DH : (h + 1) * DH])
+        two = twice(nt, high, low, vh) * same_doc
         do_high.append(high)
-        do_low.append(low)
         score_two.append(two)
-        target_own.append(nn(two_high, kh) + nn(two_low, kh))
+        target_own[:, cols] = twice(nn, *halves(two), kh)
     loads[5].wait()
     loads[6].wait()
 
@@ -245,63 +256,66 @@
     carried = jnp.where(doc_col == label_in, 1.0, 0.0).astype(F32)
     carried_two = jnp.concatenate([carried, carried], axis=0).astype(BF)
     same_two = jnp.concatenate([same_doc, same_doc], axis=0)
+
+    def solve(half):
+        slots = range(in_half)
+        cols = [cols_of(half, i) for i in slots]
+        keys, x, r, p, rr = [], [], [], [], []
+        for i in slots:
+            state = get_state(p_all, half, i)
+            value_in = state[DH:]
+            target = carried * twice(nn, *halves(do_all[:, cols[i]]), value_in) + target_own[:, cols[i]]
+            b = jnp.concatenate([q[:, cols[i]].astype(F32), target], axis=0)
+            kh = k[:, cols[i]]
+            keys.append(jnp.concatenate([kh, kh, state[:DH], state[:DH]], axis=0))
+            x.append(jnp.zeros_like(b))
+            r.append(b)
+            p.append(b)
+            rr.append(jnp.sum(b * b, axis=1, keepdims=True))
+        for number in range(CG_STEPS):
+            for i in slots:
+                kh = k[:, cols[i]]
+                p_high, p_low = halves(p[i])
+                s_high, s_low = halves(twice(nt, p_high, p_low, kh) * same_two)
+                left = jnp.concatenate([s_high, s_low, p_high * carried_two, p_low * carried_two], axis=1)
+                applied = nn(left, keys[i]) + ridge[0, half * in_half + i] * p[i]
+                step = rr[i] / (jnp.sum(p[i] * applied, axis=1, keepdims=True) + EPS)
+                x[i] = x[i] + step * p[i]
+                if number < CG_STEPS - 1:
+                    r[i] = r[i] - step * applied
+                    fresh = jnp.sum(r[i] * r[i], axis=1, keepdims=True)
+                    p[i] = r[i] + fresh / (rr[i] + EPS) * p[i]
+                    rr[i] = fresh
+        for i in slots:
+            x_all[half * in_half + i] = x[i]
+
+    solve(c)
     settle("p_mate", p_mate)
-
-    keys, x, r, p, rr = [], [], [], [], []
-    for h in range(heads):
-        cols = slice(h * DH, (h + 1) * DH)
-        kh = k[:, cols]
-        state = get_state(p_all, h)
-        value_in = state[DH:]
-        target = carried * (nn(do_high[h], value_in) + nn(do_low[h], value_in)) + target_own[h]
-        b = jnp.concatenate([q[:, cols].astype(F32), target], axis=0)
-        keys.append(jnp.concatenate([kh, state[:DH]], axis=0))
-        x.append(jnp.zeros_like(b))
-        r.append(b)
-        p.append(b)
-        rr.append(jnp.sum(b * b, axis=1, keepdims=True))
-    for number in range(CG_STEPS):
-        for h in range(heads):
-            cols = slice(h * DH, (h + 1) * DH)
-            kh = k[:, cols]
-            p_high, p_low = halves(p[h])
-            scores = (nt(p_high, kh) + nt(p_low, kh)) * same_two
-            s_high, s_low = halves(scores)
-            applied = (
-                nn(jnp.concatenate([s_high, p_high * carried_two], axis=1), keys[h])
-                + nn(jnp.concatenate([s_low, p_low * carried_two], axis=1), keys[h])
-                + ridge[0, h] * p[h]
-            )
-            step = rr[h] / (jnp.sum(p[h] * applied, axis=1, keepdims=True) + EPS)
-            x[h] = x[h] + step * p[h]
-            if number < CG_STEPS - 1:
-                r[h] = r[h] - step * applied
-                fresh = jnp.sum(r[h] * r[h], axis=1, keepdims=True)
-                p[h] = r[h] + fresh / (rr[h] + EPS) * p[h]
-                rr[h] = fresh
-
-    x_high, x_low, score_x = [], [], []
-    for h in range(heads):
-        high, low = halves(x[h])
+    solve(other)
+
+    for h, (half, i) in enumerate(order):
+        x_h = x_all[h]
+        rows_x = (head_rows * x_h[:DH]).astype(BF)
+        both = tn(jnp.concatenate([do_high[h], x_h[DH:].astype(BF)], axis=1), rows_x)
+        cross = both[DH:]
+        put_state(b_own, half, i, jnp.concatenate([both[:DH], cross + cross.T], axis=0))
+    send("b_mate", b_own.at[other], b_mate, mate)
+
+    x_high, score_x = [], []
+    for h, (half, i) in enumerate(order):
+        cols = cols_of(half, i)
+        kh, vh = k[:, cols], v[:, cols]
+        value_in = get_state(p_all, half, i)[DH:]
+        high, low = halves(x_all[h])
         x_high.append(high)
-        x_low.append(low)
-        rows_x = (head_rows * x[h][:DH]).astype(BF)
-        both = tn(jnp.concatenate([do_high[h], high[DH:]], axis=1), rows_x)
-        cross = both[DH:]
-        put_state(b_own, h, jnp.concatenate([both[:DH], cross + cross.T], axis=0))
-    send("b_mate", b_own.at[other], b_mate, mate)
-
-    for h in range(heads):
-        cols = slice(h * DH, (h + 1) * DH)
-        kh, vh = k[:, cols], v[:, cols]
-        value_in = get_state(p_all, h)[DH:]
-        scores = (nt(x_high[h], kh) + nt(x_low[h], kh)) * same_two
+        scores = twice(nt, high, low, kh) * same_two
         score_x.append(scores)
-        s_high, s_low = halves(scores[:DH])
-        out = nn(s_high, vh) + nn(s_low, vh) + carried * (nt(x_high[h][:DH], value_in) + nt(x_low[h][:DH], value_in))
-        mix[y, :, cols] = out.astype(BF)
-    for yy in y_peers:
-        send("mix", mix.at[y], mix.at[y], at(yy, z, c))
+        out = twice(nn, *halves(scores[:DH]), vh) + carried * twice(nt, high[:DH], low[:DH], value_in)
+        group = h // in_half
+        mix[group, y, :, i * DH : (i + 1) * DH] = out.astype(BF)
+        if i == in_half - 1:
+            for yy in y_peers:
+                send(f"mix{group}", mix.at[group, y], mix.at[group, y], at(yy, z, c))
 
     settle("b_mate", b_mate)
     combine(b_own, b_mate, b_send, 1, leads_back)
@@ -309,28 +323,26 @@
         send("b", b_send.at[zz], b_recv.at[z], at(y, zz, c))
     b_recv[z] = b_send[z]
 
-    for h in range(heads):
-        gq[:, h * DH : (h + 1) * DH] = x[h][DH:].astype(BF)
-    mixed = mix[y]
+    for h, (half, i) in enumerate(order):
+        gq[:, cols_of(half, i)] = x_high[h][DH:]
+    mixed = jnp.concatenate([mix[group, y] for group in range(nc)], axis=1)
+
+    def project(block):
+        cols = pl.ds(pl.multiple_of(block * width, width), width)
+        return nn(mixed, w[:, cols])
+
     for i, hh in enumerate(x_peers):
-        part = nn(mixed, w[:, pl.ds(pl.multiple_of(hh * width, width), width)])
-        l_send[i] = part.astype(BF)
+        l_send[i] = project(hh).astype(BF)
         send("l", l_send.at[i], l_recv.at[mh], me, hh)
-    l_own[...] = nn(mixed, w[:, pl.ds(pl.multiple_of(mh * width, width), width)])
+    l_own[...] = project(mh)
     l_recv[mh] = jnp.zeros((DH, width), BF)
 
-    for h in range(heads):
-        cols = slice(h * DH, (h + 1) * DH)
+    for h, (half, i) in enumerate(order):
+        cols = cols_of(half, i)
         one = score_x[h][:DH].astype(BF)
         rest = (score_two[h] - score_x[h][DH:]).astype(BF)
         gv[:, cols] = tn(one, do_high[h])
         gk[:, cols] = tn(rest, x_high[h][:DH]) - tn(one, x_high[h][DH:])
-
-    settle("b", b_recv.at[pl.ds(0, nz - 1)])
-    line_total(b_recv, b_line, 1, True)
-    for yy in y_peers:
-        send("b_line", b_line, b_lines.at[y], at(yy, z, c))
-    b_lines[y] = b_line[...]
 
     settle("cot_y", cot_y.at[pl.ds(0, ny - 1)])
     for b in range(ny):
@@ -340,23 +352,35 @@
                 cut = (zz * nc + cc) * strip
                 cot_t[cc, zz * strip : (zz + 1) * strip, b * DH : (b + 1) * DH] = turned[cut : cut + strip, :]
 
-    settle("mix", mix.at[pl.ds(0, ny - 1)])
-    gathered = mix[...].reshape(ny * DH, width)
-    gw_send[...] = nn(cot_t[other], gathered).astype(BF).reshape(nz, strip, width)
-    send("gw", gw_send, gw_recv, mate)
-    gw_own[...] = nn(cot_t[c], gathered).reshape(nz, strip, width)
+    def product(group):
+        settle(f"mix{group}", mix.at[group, pl.ds(0, ny - 1)])
+        gathered = mix[group].reshape(ny * DH, chunk)
+        gw_send[group] = nn(cot_t[other], gathered).astype(BF).reshape(nz, strip, chunk)
+        send(f"gw{group}", gw_send.at[group], gw_recv.at[group], mate)
+        gw_own[group] = nn(cot_t[c], gathered).reshape(nz, strip, chunk)
+
+    def along_z(group):
+        settle(f"gw{group}", gw_recv.at[group])
+        z_send[group] = (gw_own[group] + gw_recv[group].astype(F32)).astype(BF)
+        for zz in z_peers:
+            send(f"z{group}", z_send.at[group, zz], z_recv.at[group, z], at(y, zz, c))
+        z_recv[group, z] = z_send[group, z]
+
+    product(0)
+    settle("b", b_recv.at[pl.ds(0, nz - 1)])
+    line_total(b_recv, b_line, 1, True)
+    for yy in y_peers:
+        send("b_line", b_line, b_lines.at[y], at(yy, z, c))
+    b_lines[y] = b_line[...]
+    along_z(0)
+    product(1)
     settle("b_line", b_lines.at[pl.ds(0, ny - 1)])
     total, before = incoming(b_lines, 1, True)
     chip_before = scan(b_recv, total, before, r_send, 1, True)
     for zz in z_peers:
         send("r", r_send.at[zz], r_recv.at[z], at(y, zz, c))
     r_recv[z] = r_send[z]
-
-    settle("gw", gw_recv)
-    z_send[...] = (gw_own[...] + gw_recv[...].astype(F32)).astype(BF)
-    for zz in z_peers:
-        send("z", z_send.at[zz], z_recv.at[z], at(y, zz, c))
-    z_recv[z] = z_send[z]
+    along_z(1)
 
     settle("l", l_recv.at[pl.ds(0, nx - 1)])
     total = l_own[...]
@@ -368,20 +392,26 @@
     label_next = spread(b_own, b_mate, r_recv, r_mate, r_all, 1, chip_before, leads_back)
     send("r_mate", r_mate, r_all.at[c], mate)
     later = jnp.where(doc_col == label_next, 1.0, 0.0).astype(F32)
+
+    def finish(half):
+        for i in range(in_half):
+            cols = cols_of(half, i)
+            kh, vh = k[:, cols], v[:, cols]
+            state = get_state(r_all, half, i)
+            grad_state, gram_grad = state[:DH], state[DH:]
+            gv_out[:, cols] = (gv[:, cols] + later * nt(kh, grad_state)).astype(BF)
+            gk_out[:, cols] = (gk[:, cols] + later * (nn(vh, grad_state) - nn(kh, gram_grad))).astype(BF)
+
+    finish(c)
     settle("r_mate", r_mate)
-    for h in range(heads):
-        cols = slice(h * DH, (h + 1) * DH)
-        kh, vh = k[:, cols], v[:, cols]
-        state = get_state(r_all, h)
-        grad_state, gram_grad = state[:DH], state[DH:]
-        gv_out[:, cols] = (gv[:, cols] + later * nt(kh, grad_state)).astype(BF)
-        gk_out[:, cols] = (gk[:, cols] + later * (nn(vh, grad_state) - nn(kh, gram_grad))).astype(BF)
-
-    settle("z", z_recv.at[pl.ds(0, nz - 1)])
-    total = z_recv[0].astype(F32)
-    for b in range(1, nz):
-        total = total + z_recv[b].astype(F32)
-    gw[...] = total
+    finish(other)
+
+    for group in range(nc):
+        settle(f"z{group}", z_recv.at[group, pl.ds(0, nz - 1)])
+        total = z_recv[group, 0].astype(F32)
+        for b in range(1, nz):
+            total = total + z_recv[group, b].astype(F32)
+        gw[:, group * chunk : (group + 1) * chunk] = total
 
     for name, ref in sent:
         pltpu.make_async_copy(ref, ref, send_sem.at[sems[name]]).wait()
@@ -435,20 +465,20 @@
             pltpu.VMEM((nx, DH, width), BF),
             pltpu.VMEM((ny, DH, width), BF),
             pltpu.VMEM((nc, nz * strip, ny * DH), BF),
-            pltpu.VMEM((ny, DH, width), BF),
+            pltpu.VMEM((DH, width), F32),
+            pltpu.VMEM((DH, width), F32),
+            pltpu.VMEM((heads, 2 * DH, DH), F32),
+            pltpu.VMEM((nc, ny, DH, width // nc), BF),
             pltpu.VMEM((nx, DH, width), BF),
             pltpu.VMEM((nx, DH, width), BF),
             pltpu.VMEM((DH, width), F32),
-            pltpu.VMEM((nz, strip, width), F32),
-            pltpu.VMEM((nz, strip, width), BF),
-            pltpu.VMEM((nz, strip, width), BF),
-            pltpu.VMEM((nz, strip, width), BF),
-            pltpu.VMEM((nz, strip, width), BF),
+            pltpu.VMEM((nc, nz, strip, width // nc), F32),
+            *[pltpu.VMEM((nc, nz, strip, width // nc), BF)] * 4,
             pltpu.VMEM((DH, width), F32),
             pltpu.VMEM((DH, width), F32),
             pltpu.SemaphoreType.DMA((7,)),
-            pltpu.SemaphoreType.DMA((19,)),
-            pltpu.SemaphoreType.DMA((19,)),
+            pltpu.SemaphoreType.DMA((22,)),
+            pltpu.SemaphoreType.DMA((22,)),
         ],
         compiler_params=pltpu.CompilerParams(collective_id=0, has_side_effects=True),
     )(ridge_reg.reshape(1, -1), query_rows, key_rows, value_rows, out_weight, out_grad, doc_ids.reshape(1, -1))

time: 51.7 us -> 50.1 us (0.969)
  Pallas kernels: 50.8 us -> 49.3 us
    pallas_call x1, Pallas kernels: 49.9 us -> 48.5 us  [per_device(): pl.pallas_call(functools.partial(kernel, dims, nx), out_shape=held, in_sp...]
where the time goes in v4:
time: 50.1 us; the launch traced here: 50 us
  Pallas kernels  49.3 us (98%)
  between operations  0.64 us (1%)
    pallas_call x1, Pallas kernels, per_device(): pl.pallas_call(functools.partial(kernel, dims, nx), out_shape=held, in_sp...  48.5 us

profile of v4, /device:TPU:1, one launch (start us, length us, event | category | flops | bytes accessed | tf_op | source)
XLA Modules:
  0.0 50.0 jit_solution(10141242566665184179)
XLA Ops:
  0.6 48.5 %shard_map.110 = (bf16[128,512]{1,0:T(8,128)(2,1)S(1)}, bf16[128,512]{1,0:T(8,128)(2,1)S(1)}, bf16[128,512]{1,0:T(8,128)(2,1)S(1)}, bf16[128,512]{1,0:T(8,128)(2,1)S(1)}, f32[32,512]{1,0:T(8,128)S(1)}) custom-call(f32[1,4]{1,0:T(1,128)} %bitcast.2, bf16[128,512]{1,0:T(8,128)(2,1)} %q_in.1, bf16[128,512]{1,0:T(8,128)(2,1)} %k_in.1, bf16[128,512]{1,0:T(8,128)(2,1)} %v_in.1, ...), custom_call_target="tpu_custom_call" | custom-call | tf_op jit(solution)/shard_map/pallas_call | solution.py:445
  49.1 0.8 %shard_map.111 = (bf16[128,512]{1,0:T(8,128)(2,1)}, bf16[128,512]{1,0:T(8,128)(2,1)}, bf16[128,512]{1,0:T(8,128)(2,1)}, bf16[128,512]{1,0:T(8,128)(2,1)}, f32[32,512]{1,0:T(8,128)}) custom-call(bf16[128,512]{1,0:T(8,128)(2,1)S(1)} %get-tuple-element.10.refs_0_, bf16[128,512]{1,0:T(8,128)(2,1)S(1)} %get-tuple-element.11.refs_1_, ...), custom_call_target="tpu_custom_call" | custom-call | tf_op jit(solution)/shard_map/pallas_call | solution.py:485

commit v5 on v4

--- a/solution.py
+++ b/solution.py
@@ -44,11 +44,11 @@
     ridge_in, q_in, k_in, v_in, w_in, og_in, doc_in,
     lay, gq, gk_out, gv_out, gw,
     ridge,
-    q, k, v, w, doc, lab_own, lab_mate, lab_chip, lab, edge_own, edge,
+    q, k, v, w, doc, lab_own, lab_mate, lab_chip, lab, edge_own, edge, note_chip, note, rim_own, rim,
     t_own, t_mate, t_send, t_recv, t_line, t_lines, p_send, p_recv, p_mate, p_all,
     b_own, b_mate, b_send, b_recv, b_line, b_lines, r_send, r_recv, r_mate, r_all,
     cot, cot_y, cot_t, do_all, target_own, x_all, mix, l_send, l_recv, l_own,
-    gw_own, gw_send, gw_recv, z_send, z_recv,
+    gw_own, gw_send, gw_recv, z_send, z_far, z_add, z_recv,
     gk, gv,
     load_sem, send_sem, recv_sem,
 ):
@@ -71,8 +71,8 @@
     z_peers = [lax.rem(z + i, nz) for i in sorted(range(1, nz), key=lambda i: -min(i, nz - i))]
     x_peers = [lax.rem(mh + i, nx) for i in range(1, nx)]
 
-    names = ("lab_mate", "lab", "edge", "t_mate", "t", "t_line", "p", "p_mate", "b_mate", "b", "b_line",
-             "r", "r_mate", "cot", "cot_y", "l", "mix0", "mix1", "gw0", "gw1", "z0", "z1")
+    names = ("lab_mate", "lab", "edge", "t_mate", "t", "t_line", "p", "p_mate", "b_mate", "b", "b_line", "note", "rim",
+             "r", "r_mate", "cot", "cot_y", "l", "mix0", "mix1", "gw0", "gw1", "far0", "far1", "z0", "z1")
     sems = {name: i for i, name in enumerate(names)}
     sent = []
 
@@ -84,7 +84,10 @@
         )
         copy.start()
 
-    def settle(name, ref):
+    def settle(name, ref, count=None):
+        if count == 0:
+            return
+        ref = ref if count is None else ref.at[pl.ds(0, count)]
         sent.append((name, ref))
         pltpu.make_async_copy(ref, ref, recv_sem.at[sems[name]]).wait()
 
@@ -107,23 +110,24 @@
     doc_row = jnp.broadcast_to(doc[...].astype(F32), (DH, DH))
     doc_col = doc_row.T
     last, first = doc_col[DH - 1 : DH, :], doc_col[0:1, :]
+    for small in (lab_own, lab_chip, edge_own, note_chip, rim_own):
+        small[...] = jnp.zeros_like(small)
     lab_own[0:1, :] = last
     lab_own[1:2, :] = first
-    below = lax.broadcasted_iota(jnp.int32, (DH, DH), 1) <= lax.broadcasted_iota(jnp.int32, (DH, DH), 0)
-    same_doc = jnp.where((doc_row == doc_col) & below, 1.0, 0.0).astype(F32)
+    same_doc = jnp.where(
+        (doc_row == doc_col)
+        & (lax.broadcasted_iota(jnp.int32, (DH, DH), 1) <= lax.broadcasted_iota(jnp.int32, (DH, DH), 0)),
+        1.0,
+        0.0,
+    ).astype(F32)
     tail = jnp.where(doc_col == last, 1.0, 0.0).astype(BF)
     head_rows = jnp.where(doc_col == first, 1.0, 0.0).astype(F32)
 
     in_half = heads // nc
-    per_head = 2 * DH // rows
     chunk = in_half * DH
     order = [(half, i) for half in range(nc) for i in range(in_half)]
-
-    def put_state(ref, half, i, state):
-        ref[half, i * per_head : (i + 1) * per_head] = state.astype(BF).reshape(per_head, rows, DH)
-
-    def get_state(ref, half, i):
-        return ref[half, i * per_head : (i + 1) * per_head].reshape(2 * DH, DH)
+    row_idx = lax.broadcasted_iota(jnp.int32, (DH, DH), 0)
+    col_idx = lax.broadcasted_iota(jnp.int32, (DH, DH), 1)
 
     def cols_of(half, i):
         start = (half * in_half + i) * DH
@@ -135,54 +139,72 @@
         for i in range(in_half):
             cols = cols_of(half, i)
             kh, vh = k[:, cols], v[:, cols]
-            put_state(t_own, half, i, tn(jnp.concatenate([kh * tail, vh * tail], axis=1), kh))
+            t_own[half, i] = tn(jnp.concatenate([kh * tail, vh * tail], axis=1), kh).astype(BF)
 
     gram(other)
     loads[3].wait()
     pl.semaphore_wait(barrier, len(peers))
 
-    def combine(own, from_mate, chip, row, leads):
+    def combine(own, from_mate, packed, row, leads):
         joined = jnp.where(lab_own[row : row + 1, :] == lab_mate[row : row + 1, :], 1.0, 0.0)
         own_part = jnp.where(leads, joined, 1.0)
         mate_part = jnp.where(leads, 1.0, joined)
-        for i in range(nz):
-            chip[i] = (own[c, i].astype(F32) * own_part + from_mate[i].astype(F32) * mate_part).astype(BF)
-
-    def line_total(parts, line, row, reverse):
-        total, before = jnp.zeros((rows, DH), F32), None
+        one, two = [own[c, i].astype(F32) * own_part + from_mate[i].astype(F32) * mate_part for i in range(in_half)]
+        mixed = jnp.where(col_idx >= row_idx, one[:DH], two[:DH])
+        packed[...] = jnp.concatenate([mixed, one[DH:], two[DH:]], axis=0).astype(BF).reshape(nz, rows, DH)
+        return jnp.sum(jnp.where(col_idx == row_idx, two[:DH], 0.0), axis=0, keepdims=True)
+
+    def unpack(packed, diagonal):
+        whole = packed[...].reshape(3 * DH, DH).astype(F32)
+        mixed = whole[:DH]
+        turned = mixed.T
+        one = jnp.where(col_idx >= row_idx, mixed, turned)
+        two = jnp.where(col_idx < row_idx, mixed, jnp.where(col_idx == row_idx, diagonal, turned))
+        return jnp.concatenate([one, whole[DH : 2 * DH]], axis=0), jnp.concatenate([two, whole[2 * DH :]], axis=0)
+
+    def line_total(parts, diagonals, line, row, reverse):
+        total, diagonal, before = jnp.zeros((rows, DH), F32), jnp.zeros((1, DH), F32), None
         for i in reversed(range(nz)) if reverse else range(nz):
             label = lab[i, row : row + 1, :]
             if before is not None:
                 total = jnp.where(label == before, total, 0.0)
+                diagonal = jnp.where(label == before, diagonal, 0.0)
             total = total + parts[i].astype(F32)
+            diagonal = diagonal + diagonals[i, 2:3, :]
             before = label
         line[...] = total.astype(BF)
-
-    def incoming(lines, row, reverse):
-        total, before = jnp.zeros((rows, DH), F32), jnp.full((1, DH), -1.0, F32)
+        return diagonal
+
+    def incoming(lines, diagonals, row, reverse):
+        total, diagonal = jnp.zeros((rows, DH), F32), jnp.zeros((1, DH), F32)
+        before = jnp.full((1, DH), -1.0, F32)
         for i in reversed(range(ny)) if reverse else range(ny):
             label = edge[i, row : row + 1, :]
             grown = jnp.where(label == before, total, 0.0) + lines[i].astype(F32)
+            grown_diagonal = jnp.where(label == before, diagonal, 0.0) + diagonals[i, 2:3, :]
             reached = i > y if reverse else i < y
             total = jnp.where(reached, grown, total)
+            diagonal = jnp.where(reached, grown_diagonal, diagonal)
             before = jnp.where(reached, label, before)
-        return total, before
-
-    def scan(parts, total, before, out, row, reverse):
-        chip_before = before
+        return total, diagonal, before
+
+    def scan(parts, diagonals, start, out, row, reverse):
+        total, diagonal, before = start
+        chip_diagonal, chip_before = diagonal, before
         for i in reversed(range(nz)) if reverse else range(nz):
             label = lab[i, row : row + 1, :]
             out[i] = total.astype(BF)
             chip_before = jnp.where(i == z, before, chip_before)
+            chip_diagonal = jnp.where(i == z, diagonal, chip_diagonal)
             total = jnp.where(label == before, total, 0.0) + parts[i].astype(F32)
+            diagonal = jnp.where(label == before, diagonal, 0.0) + diagonals[i, 2:3, :]
             before = label
-        return chip_before
-
-    def spread(own, from_mate, chip, to_mate, whole, row, chip_before, leads):
+        return chip_diagonal, chip_before
+
+    def spread(own, from_mate, packed, chip_diagonal, to_mate, whole, row, chip_before, leads):
         lead_label = jnp.where(leads, lab_own[row : row + 1, :], lab_mate[row : row + 1, :])
         joined = jnp.where(lead_label == chip_before, 1.0, 0.0)
-        for i in range(nz):
-            ahead = chip[i].astype(F32)
+        for i, ahead in enumerate(unpack(packed, chip_diagonal)):
             lead_state = jnp.where(leads, own[c, i].astype(F32), from_mate[i].astype(F32))
             trail = lead_state + joined * ahead
             whole[c, i] = jnp.where(leads, ahead, trail).astype(BF)
@@ -200,36 +222,33 @@
     settle("lab_mate", lab_mate)
     lab_chip[0:1, :] = jnp.where(leads, lab_mate[0:1, :], lab_own[0:1, :])
     lab_chip[1:2, :] = jnp.where(leads, lab_own[1:2, :], lab_mate[1:2, :])
+    settle("t_mate", t_mate)
+    lab_chip[2:3, :] = combine(t_own, t_mate, t_send, 0, leads)
     lab[z] = lab_chip[...]
     for zz in z_peers:
         send("lab", lab_chip, lab.at[z], at(y, zz, c))
-    settle("t_mate", t_mate)
-    combine(t_own, t_mate, t_send, 0, leads)
-    for zz in z_peers:
         send("t", t_send.at[zz], t_recv.at[z], at(y, zz, c))
     t_recv[z] = t_send[z]
 
-    settle("lab", lab.at[pl.ds(0, nz - 1)])
+    settle("lab", lab, nz - 1)
+    settle("t", t_recv, nz - 1)
     edge_own[0:1, :] = lab[nz - 1, 0:1, :]
     edge_own[1:2, :] = lab[0, 1:2, :]
+    edge_own[2:3, :] = line_total(t_recv, lab, t_line, 0, False)
     edge[y] = edge_own[...]
     for yy in y_peers:
         send("edge", edge_own, edge.at[y], at(yy, z, c))
-    settle("t", t_recv.at[pl.ds(0, nz - 1)])
-    line_total(t_recv, t_line, 0, False)
-    for yy in y_peers:
         send("t_line", t_line, t_lines.at[y], at(yy, z, c))
     t_lines[y] = t_line[...]
-    settle("edge", edge.at[pl.ds(0, ny - 1)])
-    settle("t_line", t_lines.at[pl.ds(0, ny - 1)])
-    total, before = incoming(t_lines, 0, False)
-    chip_before = scan(t_recv, total, before, p_send, 0, False)
+    settle("edge", edge, ny - 1)
+    settle("t_line", t_lines, ny - 1)
+    chip_diagonal, chip_before = scan(t_recv, lab, incoming(t_lines, edge, 0, False), p_send, 0, False)
     for zz in z_peers:
         send("p", p_send.at[zz], p_recv.at[z], at(y, zz, c))
     p_recv[z] = p_send[z]
 
     loads[4].wait()
-    settle("cot", cot.at[pl.ds(0, nx - 1)])
+    settle("cot", cot, nx - 1)
     for yy in y_peers:
         send("cot_y", cot.at[yy], cot_y.at[y], at(yy, z, c))
     cot_y[y] = cot[y]
@@ -250,8 +269,8 @@
     loads[5].wait()
     loads[6].wait()
 
-    settle("p", p_recv.at[pl.ds(0, nz - 1)])
-    label_in = spread(t_own, t_mate, p_recv, p_mate, p_all, 0, chip_before, leads)
+    settle("p", p_recv, nz - 1)
+    label_in = spread(t_own, t_mate, p_recv, chip_diagonal, p_mate, p_all, 0, chip_before, leads)
     send("p_mate", p_mate, p_all.at[c], mate)
     carried = jnp.where(doc_col == label_in, 1.0, 0.0).astype(F32)
     carried_two = jnp.concatenate([carried, carried], axis=0).astype(BF)
@@ -262,7 +281,7 @@
         cols = [cols_of(half, i) for i in slots]
         keys, x, r, p, rr = [], [], [], [], []
         for i in slots:
-            state = get_state(p_all, half, i)
+            state = p_all[half, i]
             value_in = state[DH:]
             target = carried * twice(nn, *halves(do_all[:, cols[i]]), value_in) + target_own[:, cols[i]]
             b = jnp.concatenate([q[:, cols[i]].astype(F32), target], axis=0)
@@ -298,14 +317,14 @@
         rows_x = (head_rows * x_h[:DH]).astype(BF)
         both = tn(jnp.concatenate([do_high[h], x_h[DH:].astype(BF)], axis=1), rows_x)
         cross = both[DH:]
-        put_state(b_own, half, i, jnp.concatenate([both[:DH], cross + cross.T], axis=0))
+        b_own[half, i] = jnp.concatenate([cross + cross.T, both[:DH]], axis=0).astype(BF)
     send("b_mate", b_own.at[other], b_mate, mate)
 
     x_high, score_x = [], []
     for h, (half, i) in enumerate(order):
         cols = cols_of(half, i)
         kh, vh = k[:, cols], v[:, cols]
-        value_in = get_state(p_all, half, i)[DH:]
+        value_in = p_all[half, i, DH:, :]
         high, low = halves(x_all[h])
         x_high.append(high)
         scores = twice(nt, high, low, kh) * same_two
@@ -318,8 +337,10 @@
                 send(f"mix{group}", mix.at[group, y], mix.at[group, y], at(yy, z, c))
 
     settle("b_mate", b_mate)
-    combine(b_own, b_mate, b_send, 1, leads_back)
+    note_chip[2:3, :] = combine(b_own, b_mate, b_send, 1, leads_back)
+    note[z] = note_chip[...]
     for zz in z_peers:
+        send("note", note_chip, note.at[z], at(y, zz, c))
         send("b", b_send.at[zz], b_recv.at[z], at(y, zz, c))
     b_recv[z] = b_send[z]
 
@@ -344,7 +365,7 @@
         gv[:, cols] = tn(one, do_high[h])
         gk[:, cols] = tn(rest, x_high[h][:DH]) - tn(one, x_high[h][DH:])
 
-    settle("cot_y", cot_y.at[pl.ds(0, ny - 1)])
+    settle("cot_y", cot_y, ny - 1)
     for b in range(ny):
         turned = cot_y[b].T
         for zz in range(nz):
@@ -353,43 +374,75 @@
                 cot_t[cc, zz * strip : (zz + 1) * strip, b * DH : (b + 1) * DH] = turned[cut : cut + strip, :]
 
     def product(group):
-        settle(f"mix{group}", mix.at[group, pl.ds(0, ny - 1)])
+        settle(f"mix{group}", mix.at[group], ny - 1)
         gathered = mix[group].reshape(ny * DH, chunk)
         gw_send[group] = nn(cot_t[other], gathered).astype(BF).reshape(nz, strip, chunk)
         send(f"gw{group}", gw_send.at[group], gw_recv.at[group], mate)
         gw_own[group] = nn(cot_t[c], gathered).reshape(nz, strip, chunk)
 
+    distances = [i if i <= nz // 2 else i - nz for i in range(1, nz)]
+    near = [d for d in (1, -1, 2, -2) if d in distances]
+    far = [d for d in distances if abs(d) > 2]
+    side = jnp.where(leads, 2, -2)
+    two_away = [d for d in near if abs(d) == 2]
+
+    def chip(distance):
+        return lax.rem(z + distance + nz, nz)
+
     def along_z(group):
         settle(f"gw{group}", gw_recv.at[group])
         z_send[group] = (gw_own[group] + gw_recv[group].astype(F32)).astype(BF)
-        for zz in z_peers:
-            send(f"z{group}", z_send.at[group, zz], z_recv.at[group, z], at(y, zz, c))
-        z_recv[group, z] = z_send[group, z]
+        for slot, d in enumerate(far):
+            via = side if abs(d) == 4 else d // 3
+            send(f"far{group}", z_send.at[group, chip(d)], z_far.at[group, slot], at(y, chip(via), c))
+        for slot, d in enumerate(near):
+            if d not in two_away:
+                send(f"z{group}", z_send.at[group, chip(d)], z_recv.at[group, slot], at(y, chip(d), c))
+
+    def along_z_again(group):
+        if not two_away:
+            return
+        settle(f"far{group}", z_far.at[group])
+        for d in two_away:
+            total = z_send[group, chip(d)].astype(F32)
+            for slot, e in enumerate(far):
+                if abs(e) == 4:
+                    total = total + jnp.where(side == d, z_far[group, slot].astype(F32), 0.0)
+                elif e * d > 0:
+                    total = total + z_far[group, slot].astype(F32)
+            z_add[group, two_away.index(d)] = total.astype(BF)
+            slot = near.index(d)
+            send(f"z{group}", z_add.at[group, two_away.index(d)], z_recv.at[group, slot], at(y, chip(d), c))
 
     product(0)
-    settle("b", b_recv.at[pl.ds(0, nz - 1)])
-    line_total(b_recv, b_line, 1, True)
+    settle("note", note, nz - 1)
+    settle("b", b_recv, nz - 1)
+    rim_own[2:3, :] = line_total(b_recv, note, b_line, 1, True)
+    rim[y] = rim_own[...]
     for yy in y_peers:
+        send("rim", rim_own, rim.at[y], at(yy, z, c))
         send("b_line", b_line, b_lines.at[y], at(yy, z, c))
     b_lines[y] = b_line[...]
     along_z(0)
     product(1)
-    settle("b_line", b_lines.at[pl.ds(0, ny - 1)])
-    total, before = incoming(b_lines, 1, True)
-    chip_before = scan(b_recv, total, before, r_send, 1, True)
+    along_z(1)
+    settle("rim", rim, ny - 1)
+    settle("b_line", b_lines, ny - 1)
+    chip_diagonal, chip_before = scan(b_recv, note, incoming(b_lines, rim, 1, True), r_send, 1, True)
     for zz in z_peers:
         send("r", r_send.at[zz], r_recv.at[z], at(y, zz, c))
     r_recv[z] = r_send[z]
-    along_z(1)
-
-    settle("l", l_recv.at[pl.ds(0, nx - 1)])
+
+    along_z_again(0)
+    settle("l", l_recv, nx - 1)
     total = l_own[...]
     for b in range(nx):
         total = total + l_recv[b].astype(F32)
     lay[...] = total.astype(BF)
-
-    settle("r", r_recv.at[pl.ds(0, nz - 1)])
-    label_next = spread(b_own, b_mate, r_recv, r_mate, r_all, 1, chip_before, leads_back)
+    along_z_again(1)
+
+    settle("r", r_recv, nz - 1)
+    label_next = spread(b_own, b_mate, r_recv, chip_diagonal, r_mate, r_all, 1, chip_before, leads_back)
     send("r_mate", r_mate, r_all.at[c], mate)
     later = jnp.where(doc_col == label_next, 1.0, 0.0).astype(F32)
 
@@ -397,8 +450,8 @@
         for i in range(in_half):
             cols = cols_of(half, i)
             kh, vh = k[:, cols], v[:, cols]
-            state = get_state(r_all, half, i)
-            grad_state, gram_grad = state[:DH], state[DH:]
+            state = r_all[half, i]
+            gram_grad, grad_state = state[:DH], state[DH:]
             gv_out[:, cols] = (gv[:, cols] + later * nt(kh, grad_state)).astype(BF)
             gk_out[:, cols] = (gk[:, cols] + later * (nn(vh, grad_state) - nn(kh, gram_grad))).astype(BF)
 
@@ -407,10 +460,10 @@
     finish(other)
 
     for group in range(nc):
-        settle(f"z{group}", z_recv.at[group, pl.ds(0, nz - 1)])
-        total = z_recv[group, 0].astype(F32)
-        for b in range(1, nz):
-            total = total + z_recv[group, b].astype(F32)
+        settle(f"z{group}", z_recv.at[group])
+        total = z_send[group, z].astype(F32)
+        for slot in range(len(near)):
+            total = total + z_recv[group, slot].astype(F32)
         gw[:, group * chunk : (group + 1) * chunk] = total
 
     for name, ref in sent:
@@ -431,17 +484,18 @@
     ny, nz, nc = dims
     heads = ridge_reg.shape[0]
     width = heads * DH
-    rows = heads * 2 * DH // (nc * nz)
+    rows = 3 * DH // nz
     strip = width // (nz * nc)
     any_space = pl.BlockSpec(memory_space=pl.ANY)
-    half = pltpu.VMEM((nz, rows, DH), BF)
-    both = pltpu.VMEM((nc, nz, rows, DH), BF)
+    packed = pltpu.VMEM((nz, rows, DH), BF)
+    half = pltpu.VMEM((heads // nc, 2 * DH, DH), BF)
+    both = pltpu.VMEM((nc, heads // nc, 2 * DH, DH), BF)
     line = pltpu.VMEM((rows, DH), BF)
     lines = pltpu.VMEM((ny, rows, DH), BF)
-    label = pltpu.VMEM((2, DH), F32)
+    label = pltpu.VMEM((4, DH), F32)
     wide = pltpu.VMEM((DH, width), BF)
     held = (wide, wide, wide, wide, pltpu.VMEM((strip, width), F32))
-    states = [both, half, half, half, line, lines, half, half, half, both]
+    states = [both, half, packed, packed, line, lines, packed, packed, half, both]
     made = pl.pallas_call(
         functools.partial(kernel, dims, nx),
         out_shape=held,
@@ -457,9 +511,13 @@
             label,
             label,
             label,
-            pltpu.VMEM((nz, 2, DH), F32),
+            pltpu.VMEM((nz, 4, DH), F32),
             label,
-            pltpu.VMEM((ny, 2, DH), F32),
+            pltpu.VMEM((ny, 4, DH), F32),
+            label,
+            pltpu.VMEM((nz, 4, DH), F32),
+            label,
+            pltpu.VMEM((ny, 4, DH), F32),
             *states,
             *states,
             pltpu.VMEM((nx, DH, width), BF),
@@ -473,12 +531,15 @@
             pltpu.VMEM((nx, DH, width), BF),
             pltpu.VMEM((DH, width), F32),
             pltpu.VMEM((nc, nz, strip, width // nc), F32),
-            *[pltpu.VMEM((nc, nz, strip, width // nc), BF)] * 4,
+            *[pltpu.VMEM((nc, nz, strip, width // nc), BF)] * 3,
+            pltpu.VMEM((nc, 3, strip, width // nc), BF),
+            pltpu.VMEM((nc, 2, strip, width // nc), BF),
+            pltpu.VMEM((nc, min(4, nz - 1), strip, width // nc), BF),
             pltpu.VMEM((DH, width), F32),
             pltpu.VMEM((DH, width), F32),
             pltpu.SemaphoreType.DMA((7,)),
-            pltpu.SemaphoreType.DMA((22,)),
-            pltpu.SemaphoreType.DMA((22,)),
+            pltpu.SemaphoreType.DMA((26,)),
+            pltpu.SemaphoreType.DMA((26,)),
         ],
         compiler_params=pltpu.CompilerParams(collective_id=0, has_side_effects=True),
     )(ridge_reg.reshape(1, -1), query_rows, key_rows, value_rows, out_weight, out_grad, doc_ids.reshape(1, -1))

time: 50.1 us -> 47.8 us (0.954)
  Pallas kernels: 49.3 us -> 47.1 us
    pallas_call x1, Pallas kernels: 48.5 us -> 46.3 us  [per_device(): pl.pallas_call(functools.partial(kernel, dims, nx), out_shape=held, in_sp...]
where the time goes in v5:
time: 47.8 us; the launch traced here: 47.7 us
  Pallas kernels  47.1 us (99%)
  between operations  0.64 us (1%)
    pallas_call x1, Pallas kernels, per_device(): pl.pallas_call(functools.partial(kernel, dims, nx), out_shape=held, in_sp...  46.3 us

profile of v5, /device:TPU:1, one launch (start us, length us, event | category | flops | bytes accessed | tf_op | source)
XLA Modules:
  0.0 47.7 jit_solution(17253456993096245513)
XLA Ops:
  0.6 46.3 %shard_map.110 = (bf16[128,512]{1,0:T(8,128)(2,1)S(1)}, bf16[128,512]{1,0:T(8,128)(2,1)S(1)}, bf16[128,512]{1,0:T(8,128)(2,1)S(1)}, bf16[128,512]{1,0:T(8,128)(2,1)S(1)}, f32[32,512]{1,0:T(8,128)S(1)}) custom-call(f32[1,4]{1,0:T(1,128)} %bitcast.2, bf16[128,512]{1,0:T(8,128)(2,1)} %q_in.1, bf16[128,512]{1,0:T(8,128)(2,1)} %k_in.1, bf16[128,512]{1,0:T(8,128)(2,1)} %v_in.1, ...), custom_call_target="tpu_custom_call" | custom-call | tf_op jit(solution)/shard_map/pallas_call | solution.py:499
  46.9 0.8 %shard_map.111 = (bf16[128,512]{1,0:T(8,128)(2,1)}, bf16[128,512]{1,0:T(8,128)(2,1)}, bf16[128,512]{1,0:T(8,128)(2,1)}, bf16[128,512]{1,0:T(8,128)(2,1)}, f32[32,512]{1,0:T(8,128)}) custom-call(bf16[128,512]{1,0:T(8,128)(2,1)S(1)} %get-tuple-element.10.refs_0_, bf16[128,512]{1,0:T(8,128)(2,1)S(1)} %get-tuple-element.11.refs_1_, ...), custom_call_target="tpu_custom_call" | custom-call | tf_op jit(solution)/shard_map/pallas_call | solution.py:546

commit v6 on v5

--- a/solution.py
+++ b/solution.py
@@ -276,41 +276,44 @@
     carried_two = jnp.concatenate([carried, carried], axis=0).astype(BF)
     same_two = jnp.concatenate([same_doc, same_doc], axis=0)
 
-    def solve(half):
-        slots = range(in_half)
-        cols = [cols_of(half, i) for i in slots]
+    def solve():
+        slots = range(heads)
+        cols = [cols_of(*order[i]) for i in slots]
         keys, x, r, p, rr = [], [], [], [], []
         for i in slots:
-            state = p_all[half, i]
+            state = p_all[order[i]]
             value_in = state[DH:]
             target = carried * twice(nn, *halves(do_all[:, cols[i]]), value_in) + target_own[:, cols[i]]
             b = jnp.concatenate([q[:, cols[i]].astype(F32), target], axis=0)
             kh = k[:, cols[i]]
-            keys.append(jnp.concatenate([kh, kh, state[:DH], state[:DH]], axis=0))
+            keys.append(jnp.concatenate([kh, state[:DH]], axis=0))
             x.append(jnp.zeros_like(b))
             r.append(b)
             p.append(b)
             rr.append(jnp.sum(b * b, axis=1, keepdims=True))
         for number in range(CG_STEPS):
+            high = [p[i].astype(BF) for i in slots]
+            scores = [nt(high[i], k[:, cols[i]]) * same_two for i in slots]
+            applied = [
+                nn(jnp.concatenate([scores[i].astype(BF), high[i] * carried_two], axis=1), keys[i])
+                + ridge[0, i] * p[i]
+                for i in slots
+            ]
+            step = [rr[i] / (jnp.sum(p[i] * applied[i], axis=1, keepdims=True) + EPS) for i in slots]
             for i in slots:
-                kh = k[:, cols[i]]
-                p_high, p_low = halves(p[i])
-                s_high, s_low = halves(twice(nt, p_high, p_low, kh) * same_two)
-                left = jnp.concatenate([s_high, s_low, p_high * carried_two, p_low * carried_two], axis=1)
-                applied = nn(left, keys[i]) + ridge[0, half * in_half + i] * p[i]
-                step = rr[i] / (jnp.sum(p[i] * applied, axis=1, keepdims=True) + EPS)
-                x[i] = x[i] + step * p[i]
-                if number < CG_STEPS - 1:
-                    r[i] = r[i] - step * applied
-                    fresh = jnp.sum(r[i] * r[i], axis=1, keepdims=True)
-                    p[i] = r[i] + fresh / (rr[i] + EPS) * p[i]
-                    rr[i] = fresh
+                x[i] = x[i] + step[i] * p[i]
+            if number < CG_STEPS - 1:
+                for i in slots:
+                    r[i] = r[i] - step[i] * applied[i]
+                fresh = [jnp.sum(r[i] * r[i], axis=1, keepdims=True) for i in slots]
+                for i in slots:
+                    p[i] = r[i] + fresh[i] / (rr[i] + EPS) * p[i]
+                rr = fresh
         for i in slots:
-            x_all[half * in_half + i] = x[i]
-
-    solve(c)
+            x_all[i] = x[i]
+
     settle("p_mate", p_mate)
-    solve(other)
+    solve()
 
     for h, (half, i) in enumerate(order):
         x_h = x_all[h]

time: 47.8 us -> 47.3 us (0.990)
  Pallas kernels: 47.1 us -> 46.6 us
    pallas_call x1, Pallas kernels: 46.3 us -> 45.7 us  [per_device(): pl.pallas_call(functools.partial(kernel, dims, nx), out_shape=held, in_sp...]
where the time goes in v6:
time: 47.3 us; the launch traced here: 47.2 us
  Pallas kernels  46.6 us (99%)
  between operations  0.64 us (1%)
    pallas_call x1, Pallas kernels, per_device(): pl.pallas_call(functools.partial(kernel, dims, nx), out_shape=held, in_sp...  45.7 us

profile of v6, /device:TPU:1, one launch (start us, length us, event | category | flops | bytes accessed | tf_op | source)
XLA Modules:
  0.0 47.2 jit_solution(11902045056411981156)
XLA Ops:
  0.6 45.7 %shard_map.110 = (bf16[128,512]{1,0:T(8,128)(2,1)S(1)}, bf16[128,512]{1,0:T(8,128)(2,1)S(1)}, bf16[128,512]{1,0:T(8,128)(2,1)S(1)}, bf16[128,512]{1,0:T(8,128)(2,1)S(1)}, f32[32,512]{1,0:T(8,128)S(1)}) custom-call(f32[1,4]{1,0:T(1,128)} %bitcast.2, bf16[128,512]{1,0:T(8,128)(2,1)} %q_in.1, bf16[128,512]{1,0:T(8,128)(2,1)} %k_in.1, bf16[128,512]{1,0:T(8,128)(2,1)} %v_in.1, ...), custom_call_target="tpu_custom_call" | custom-call | tf_op jit(solution)/shard_map/pallas_call | solution.py:502
  46.4 0.8 %shard_map.111 = (bf16[128,512]{1,0:T(8,128)(2,1)}, bf16[128,512]{1,0:T(8,128)(2,1)}, bf16[128,512]{1,0:T(8,128)(2,1)}, bf16[128,512]{1,0:T(8,128)(2,1)}, f32[32,512]{1,0:T(8,128)}) custom-call(bf16[128,512]{1,0:T(8,128)(2,1)S(1)} %get-tuple-element.10.refs_0_, bf16[128,512]{1,0:T(8,128)(2,1)S(1)} %get-tuple-element.11.refs_1_, ...), custom_call_target="tpu_custom_call" | custom-call | tf_op jit(solution)/shard_map/pallas_call | solution.py:549

commit v7 on v6

--- a/solution.py
+++ b/solution.py
@@ -324,21 +324,23 @@
     send("b_mate", b_own.at[other], b_mate, mate)
 
     x_high, score_x = [], []
-    for h, (half, i) in enumerate(order):
-        cols = cols_of(half, i)
-        kh, vh = k[:, cols], v[:, cols]
-        value_in = p_all[half, i, DH:, :]
-        high, low = halves(x_all[h])
-        x_high.append(high)
-        scores = twice(nt, high, low, kh) * same_two
-        score_x.append(scores)
-        out = twice(nn, *halves(scores[:DH]), vh) + carried * twice(nt, high[:DH], low[:DH], value_in)
-        group = h // in_half
-        mix[group, y, :, i * DH : (i + 1) * DH] = out.astype(BF)
-        if i == in_half - 1:
-            for yy in y_peers:
-                send(f"mix{group}", mix.at[group, y], mix.at[group, y], at(yy, z, c))
-
+
+    def read_out(group):
+        for i in range(in_half):
+            h = group * in_half + i
+            cols = slice(h * DH, (h + 1) * DH)
+            kh, vh = k[:, cols], v[:, cols]
+            value_in = p_all[group, i, DH:, :]
+            high, low = halves(x_all[h])
+            x_high.append(high)
+            scores = twice(nt, high, low, kh) * same_two
+            score_x.append(scores)
+            out = twice(nn, *halves(scores[:DH]), vh) + carried * twice(nt, high[:DH], low[:DH], value_in)
+            mix[group, y, :, i * DH : (i + 1) * DH] = out.astype(BF)
+        for yy in y_peers:
+            send(f"mix{group}", mix.at[group, y], mix.at[group, y], at(yy, z, c))
+
+    read_out(0)
     settle("b_mate", b_mate)
     note_chip[2:3, :] = combine(b_own, b_mate, b_send, 1, leads_back)
     note[z] = note_chip[...]
@@ -347,6 +349,8 @@
         send("b", b_send.at[zz], b_recv.at[z], at(y, zz, c))
     b_recv[z] = b_send[z]
 
+    read_out(1)
+
     for h, (half, i) in enumerate(order):
         gq[:, cols_of(half, i)] = x_high[h][DH:]
     mixed = jnp.concatenate([mix[group, y] for group in range(nc)], axis=1)
@@ -386,7 +390,6 @@
     distances = [i if i <= nz // 2 else i - nz for i in range(1, nz)]
     near = [d for d in (1, -1, 2, -2) if d in distances]
     far = [d for d in distances if abs(d) > 2]
-    side = jnp.where(leads, 2, -2)
     two_away = [d for d in near if abs(d) == 2]
 
     def chip(distance):
@@ -396,7 +399,7 @@
         settle(f"gw{group}", gw_recv.at[group])
         z_send[group] = (gw_own[group] + gw_recv[group].astype(F32)).astype(BF)
         for slot, d in enumerate(far):
-            via = side if abs(d) == 4 else d // 3
+            via = -2 if abs(d) == 4 else d // 3
             send(f"far{group}", z_send.at[group, chip(d)], z_far.at[group, slot], at(y, chip(via), c))
         for slot, d in enumerate(near):
             if d not in two_away:
@@ -409,9 +412,7 @@
         for d in two_away:
             total = z_send[group, chip(d)].astype(F32)
             for slot, e in enumerate(far):
-                if abs(e) == 4:
-                    total = total + jnp.where(side == d, z_far[group, slot].astype(F32), 0.0)
-                elif e * d > 0:
+                if (d == -2) if abs(e) == 4 else (e * d > 0):
                     total = total + z_far[group, slot].astype(F32)
             z_add[group, two_away.index(d)] = total.astype(BF)
             slot = near.index(d)

time: 47.3 us -> 46.9 us (level)
  no operation moved by 1% of the time
where the time goes in v7:
time: 46.9 us; the launch traced here: 46.8 us
  Pallas kernels  46.2 us (99%)
  between operations  0.64 us (1%)
    pallas_call x1, Pallas kernels, per_device(): pl.pallas_call(functools.partial(kernel, dims, nx), out_shape=held, in_sp...  45.3 us

profile of v7, /device:TPU:1, one launch (start us, length us, event | category | flops | bytes accessed | tf_op | source)
XLA Modules:
  0.0 46.8 jit_solution(8877992183916833966)
XLA Ops:
  0.6 45.3 %shard_map.110 = (bf16[128,512]{1,0:T(8,128)(2,1)S(1)}, bf16[128,512]{1,0:T(8,128)(2,1)S(1)}, bf16[128,512]{1,0:T(8,128)(2,1)S(1)}, bf16[128,512]{1,0:T(8,128)(2,1)S(1)}, f32[32,512]{1,0:T(8,128)S(1)}) custom-call(f32[1,4]{1,0:T(1,128)} %bitcast.2, bf16[128,512]{1,0:T(8,128)(2,1)} %q_in.1, bf16[128,512]{1,0:T(8,128)(2,1)} %k_in.1, bf16[128,512]{1,0:T(8,128)(2,1)} %v_in.1, ...), custom_call_target="tpu_custom_call" | custom-call | tf_op jit(solution)/shard_map/pallas_call | solution.py:503
  46.0 0.8 %shard_map.111 = (bf16[128,512]{1,0:T(8,128)(2,1)}, bf16[128,512]{1,0:T(8,128)(2,1)}, bf16[128,512]{1,0:T(8,128)(2,1)}, bf16[128,512]{1,0:T(8,128)(2,1)}, f32[32,512]{1,0:T(8,128)}) custom-call(bf16[128,512]{1,0:T(8,128)(2,1)S(1)} %get-tuple-element.10.refs_0_, bf16[128,512]{1,0:T(8,128)(2,1)S(1)} %get-tuple-element.11.refs_1_, ...), custom_call_target="tpu_custom_call" | custom-call | tf_op jit(solution)/shard_map/pallas_call | solution.py:550

commit v8 on v7

--- a/solution.py
+++ b/solution.py
@@ -401,11 +401,11 @@
         for slot, d in enumerate(far):
             via = -2 if abs(d) == 4 else d // 3
             send(f"far{group}", z_send.at[group, chip(d)], z_far.at[group, slot], at(y, chip(via), c))
+
+    def along_z_again(group):
         for slot, d in enumerate(near):
             if d not in two_away:
                 send(f"z{group}", z_send.at[group, chip(d)], z_recv.at[group, slot], at(y, chip(d), c))
-
-    def along_z_again(group):
         if not two_away:
             return
         settle(f"far{group}", z_far.at[group])

time: 46.9 us -> 46.6 us (level)
  no operation moved by 1% of the time
where the time goes in v8:
time: 46.6 us; the launch traced here: 46.5 us
  Pallas kernels  45.9 us (98%)
  between operations  0.64 us (1%)
    pallas_call x1, Pallas kernels, per_device(): pl.pallas_call(functools.partial(kernel, dims, nx), out_shape=held, in_sp...  45 us

profile of v8, /device:TPU:1, one launch (start us, length us, event | category | flops | bytes accessed | tf_op | source)
XLA Modules:
  0.0 46.5 jit_solution(5914216552691391309)
XLA Ops:
  0.6 45.0 %shard_map.110 = (bf16[128,512]{1,0:T(8,128)(2,1)S(1)}, bf16[128,512]{1,0:T(8,128)(2,1)S(1)}, bf16[128,512]{1,0:T(8,128)(2,1)S(1)}, bf16[128,512]{1,0:T(8,128)(2,1)S(1)}, f32[32,512]{1,0:T(8,128)S(1)}) custom-call(f32[1,4]{1,0:T(1,128)} %bitcast.2, bf16[128,512]{1,0:T(8,128)(2,1)} %q_in.1, bf16[128,512]{1,0:T(8,128)(2,1)} %k_in.1, bf16[128,512]{1,0:T(8,128)(2,1)} %v_in.1, ...), custom_call_target="tpu_custom_call" | custom-call | tf_op jit(solution)/shard_map/pallas_call | solution.py:503
  45.6 0.8 %shard_map.111 = (bf16[128,512]{1,0:T(8,128)(2,1)}, bf16[128,512]{1,0:T(8,128)(2,1)}, bf16[128,512]{1,0:T(8,128)(2,1)}, bf16[128,512]{1,0:T(8,128)(2,1)}, f32[32,512]{1,0:T(8,128)}) custom-call(bf16[128,512]{1,0:T(8,128)(2,1)S(1)} %get-tuple-element.10.refs_0_, bf16[128,512]{1,0:T(8,128)(2,1)S(1)} %get-tuple-element.11.refs_1_, ...), custom_call_target="tpu_custom_call" | custom-call | tf_op jit(solution)/shard_map/pallas_call | solution.py:550

commit v9 on v8

--- a/solution.py
+++ b/solution.py
@@ -395,17 +395,23 @@
     def chip(distance):
         return lax.rem(z + distance + nz, nz)
 
+    def send_near(group):
+        for slot, d in enumerate(near):
+            if d not in two_away:
+                send(f"z{group}", z_send.at[group, chip(d)], z_recv.at[group, slot], at(y, chip(d), c))
+
     def along_z(group):
         settle(f"gw{group}", gw_recv.at[group])
         z_send[group] = (gw_own[group] + gw_recv[group].astype(F32)).astype(BF)
         for slot, d in enumerate(far):
             via = -2 if abs(d) == 4 else d // 3
             send(f"far{group}", z_send.at[group, chip(d)], z_far.at[group, slot], at(y, chip(via), c))
+        if group == 0:
+            send_near(group)
 
     def along_z_again(group):
-        for slot, d in enumerate(near):
-            if d not in two_away:
-                send(f"z{group}", z_send.at[group, chip(d)], z_recv.at[group, slot], at(y, chip(d), c))
+        if group > 0:
+            send_near(group)
         if not two_away:
             return
         settle(f"far{group}", z_far.at[group])

time: 46.6 us -> 46.3 us (level)
  no operation moved by 1% of the time
where the time goes in v9:
time: 46.3 us; the launch traced here: 46.2 us
  Pallas kernels  45.6 us (98%)
  between operations  0.64 us (1%)
    pallas_call x1, Pallas kernels, per_device(): pl.pallas_call(functools.partial(kernel, dims, nx), out_shape=held, in_sp...  44.8 us

profile of v9, /device:TPU:1, one launch (start us, length us, event | category | flops | bytes accessed | tf_op | source)
XLA Modules:
  0.0 46.2 jit_solution(1689257492503365485)
XLA Ops:
  0.6 44.8 %shard_map.110 = (bf16[128,512]{1,0:T(8,128)(2,1)S(1)}, bf16[128,512]{1,0:T(8,128)(2,1)S(1)}, bf16[128,512]{1,0:T(8,128)(2,1)S(1)}, bf16[128,512]{1,0:T(8,128)(2,1)S(1)}, f32[32,512]{1,0:T(8,128)S(1)}) custom-call(f32[1,4]{1,0:T(1,128)} %bitcast.2, bf16[128,512]{1,0:T(8,128)(2,1)} %q_in.1, bf16[128,512]{1,0:T(8,128)(2,1)} %k_in.1, bf16[128,512]{1,0:T(8,128)(2,1)} %v_in.1, ...), custom_call_target="tpu_custom_call" | custom-call | tf_op jit(solution)/shard_map/pallas_call | solution.py:509
  45.4 0.8 %shard_map.111 = (bf16[128,512]{1,0:T(8,128)(2,1)}, bf16[128,512]{1,0:T(8,128)(2,1)}, bf16[128,512]{1,0:T(8,128)(2,1)}, bf16[128,512]{1,0:T(8,128)(2,1)}, f32[32,512]{1,0:T(8,128)}) custom-call(bf16[128,512]{1,0:T(8,128)(2,1)S(1)} %get-tuple-element.10.refs_0_, bf16[128,512]{1,0:T(8,128)(2,1)S(1)} %get-tuple-element.11.refs_1_, ...), custom_call_target="tpu_custom_call" | custom-call | tf_op jit(solution)/shard_map/pallas_call | solution.py:556
